TPU v7x, 512 devices: a whole 4x8x8 slice. The times are simulated.
512 devices in a mesh: blk: 64 (over y, x, core), pts: 8 (over z).
Axes of the slice: x: 4, y: 8, z: 8, core: 2. Of those that a mesh axis runs over, the one named last changes fastest.
Arguments:
- snapshots: float32 [16384, 5, 1024], P('blk', None, 'pts'), may hold values from -150 to 150
- weights: float32 [5, 1024], P(None, 'pts'), may hold values from 0.3 to 3
- offsets: int32 [64], replicated, may hold values from 0 to 255, as said below
- freqs: int32 [64], replicated, may hold values from 1 to 127, as said below
Outputs:
- modes: float32 [64, 64, 2, 5, 1024], P('blk', None, None, None, 'pts')
- spectrum: float32 [64, 64], P('blk')
Inputs may be any that keep to these rules, and one draw needn't show every extreme that they name: Block b covers snapshots b * 256 + offsets[b] onward, 256 of them; the last block's offset is 0 and some other block's is 255. `freqs`: distinct and increasing; 1 and 127 are among them.
All inputs are finite; a program needn't handle non-finite values.
Results may differ from a plain program's by a relative error of at most 0.008.
Values sent between devices are 32-bit elements; how exact they have to be, the bound alone decides.
No kernel may reach another device: no remote copies, remote signals or barrier semaphores. Data moves between devices by JAX's collectives and lax.ppermute only.
A program may use at most 64 MiB of HBM per device.

v0:
```python
import math

import jax
import jax.numpy as jnp
from jax import lax
from jax.sharding import PartitionSpec as P

SWEEPS = 2


HIGH = lax.Precision.HIGHEST
DAMPING = 0.01


def passed_along(block, axis, distance):
    devices = range(lax.axis_size(axis))
    route = [(i - distance, i) for i in devices if i - distance in devices]
    return lax.ppermute(block, axis, route)


def spectral_table(freqs, lags, valid, nfft):
    phase_index = jnp.mod(freqs[:, None] * lags[None, :], nfft)
    angle = 2.0 * math.pi / nfft * phase_index.astype(jnp.float32)
    hann = 0.5 - 0.5 * jnp.cos(2.0 * math.pi / nfft * lags.astype(jnp.float32))
    factor = jnp.where(valid, hann, 0.0) / math.sqrt(nfft)
    table = jnp.stack([factor[None, :] * jnp.cos(angle), -factor[None, :] * jnp.sin(angle)], axis=1)
    return table.reshape(2 * freqs.shape[0], nfft)


def rotate_round(carry, round_index):
    real_a, imag_a, real_v, imag_v = carry
    count = real_a.shape[-1]
    index = jnp.arange(count, dtype=jnp.int32)
    mirror = jnp.mod(2 * round_index - index, count - 1)
    partner = jnp.where(
        index == count - 1, round_index, jnp.where(index == round_index, count - 1, mirror)
    )
    parity = jnp.where(index < partner, 1.0, -1.0).astype(jnp.float32)
    diagonal = jnp.diagonal(real_a, axis1=-2, axis2=-1)
    diag_pair = jnp.take(diagonal, partner, axis=-1)
    columns = jnp.broadcast_to(partner[:, None], real_a.shape[:-1] + (1,))
    pair_real = jnp.take_along_axis(real_a, columns, axis=-1)[..., 0]
    pair_imag = jnp.take_along_axis(imag_a, columns, axis=-1)[..., 0]
    delta = parity * (diag_pair - diagonal)
    size_sq = pair_real * pair_real + pair_imag * pair_imag
    radius = jnp.sqrt(delta * delta + 4.0 * size_sq)
    upper = radius + delta + DAMPING * (diagonal + diag_pair)
    length = jnp.sqrt(upper * upper + 4.0 * size_sq)
    cosine = upper / length
    off_real = 2.0 * parity * pair_real / length
    off_imag = 2.0 * parity * pair_imag / length
    moved_real = jnp.take(off_real, partner, axis=-1)
    moved_imag = jnp.take(off_imag, partner, axis=-1)

    def right_apply(left_real, left_imag):
        swap_real = jnp.take(left_real, partner, axis=-1)
        swap_imag = jnp.take(left_imag, partner, axis=-1)
        coef_c = cosine[..., None, :]
        coef_r = moved_real[..., None, :]
        coef_i = moved_imag[..., None, :]
        return (
            left_real * coef_c + swap_real * coef_r - swap_imag * coef_i,
            left_imag * coef_c + swap_real * coef_i + swap_imag * coef_r,
        )

    half_real, half_imag = right_apply(real_a, imag_a)
    swap_real = jnp.take(half_real, partner, axis=-2)
    swap_imag = jnp.take(half_imag, partner, axis=-2)
    coef_c = cosine[..., :, None]
    coef_r = moved_real[..., :, None]
    coef_i = moved_imag[..., :, None]
    new_real = half_real * coef_c + swap_real * coef_r + swap_imag * coef_i
    new_imag = half_imag * coef_c + swap_imag * coef_r - swap_real * coef_i
    vec_real, vec_imag = right_apply(real_v, imag_v)
    return (new_real, new_imag, vec_real, vec_imag)


def jacobi_solve(gram_real, gram_imag):
    count = gram_real.shape[-1]
    identity = jnp.broadcast_to(jnp.eye(count, dtype=gram_real.dtype), gram_real.shape)
    state = (gram_real, gram_imag, identity, jnp.zeros_like(gram_real))

    def advance(counter, carry):
        return rotate_round(carry, jnp.mod(counter, count - 1).astype(jnp.int32))

    return lax.fori_loop(0, SWEEPS * (count - 1), advance, state)


def mode_factors(real_a, real_v, imag_v, nblocks):
    eigen = jnp.diagonal(real_a, axis1=-2, axis2=-1)
    sum_real = jnp.sum(real_v, axis=-2)
    sum_imag = jnp.sum(imag_v, axis=-2)
    magnitude = jnp.sqrt(sum_real * sum_real + sum_imag * sum_imag)
    scaling = 1.0 / (jnp.maximum(magnitude, 1.0) * jnp.sqrt(nblocks * (eigen + 1e-06)))
    phase_real = (sum_real * scaling)[..., None, :]
    phase_imag = (-sum_imag * scaling)[..., None, :]
    coef_real = real_v * phase_real - imag_v * phase_imag
    coef_imag = real_v * phase_imag + imag_v * phase_real
    return (eigen, coef_real, coef_imag)


def body(snapshots, weights, offsets, freqs):
    nfft, nvars, npts = snapshots.shape
    nfreq = freqs.shape[0]
    nblocks = lax.axis_size("blk")
    total_pts = npts * lax.axis_size("pts")
    width = nvars * npts
    block = lax.axis_index("blk")
    lags = jnp.arange(nfft, dtype=jnp.int32)
    flat = snapshots.reshape(nfft, width)
    own_off = offsets[block]
    own_table = spectral_table(freqs, lags - own_off, lags >= own_off, nfft)
    spectra = jnp.dot(own_table, flat, precision=HIGH)
    following = passed_along(flat, "blk", -1)
    tail_table = spectral_table(freqs, lags + nfft - own_off, lags < own_off, nfft)
    spectra = spectra + jnp.dot(tail_table, following, precision=HIGH)
    spectra = spectra.reshape(nfreq, 2, nvars, npts)
    gram_scale = 1.0 / (nblocks * nvars * total_pts)
    grouped = lax.all_to_all(spectra[:, None], "blk", split_axis=0, concat_axis=1, tiled=True)
    local_freqs = grouped.shape[0]
    part_real = grouped[:, :, 0].reshape(local_freqs, nblocks, width)
    part_imag = grouped[:, :, 1].reshape(local_freqs, nblocks, width)
    flat_weights = weights.reshape(1, 1, width)
    weighted_real = part_real * flat_weights
    weighted_imag = part_imag * flat_weights
    gram_real = (
        jnp.einsum("fbx,fcx->fbc", weighted_real, part_real, precision=HIGH)
        + jnp.einsum("fbx,fcx->fbc", weighted_imag, part_imag, precision=HIGH)
    ) * gram_scale
    gram_imag = (
        jnp.einsum("fbx,fcx->fbc", weighted_real, part_imag, precision=HIGH)
        - jnp.einsum("fbx,fcx->fbc", weighted_imag, part_real, precision=HIGH)
    ) * gram_scale
    gram_real, gram_imag = lax.psum((gram_real, gram_imag), "pts")
    real_a, imag_a, real_v, imag_v = jacobi_solve(gram_real, gram_imag)
    eigen, coef_real, coef_imag = mode_factors(real_a, real_v, imag_v, nblocks)
    total = lax.psum(jnp.sum(eigen), "blk")
    mode_real = jnp.einsum("fbx,fbm->fmx", part_real, coef_real, precision=HIGH) - jnp.einsum(
        "fbx,fbm->fmx", part_imag, coef_imag, precision=HIGH
    )
    mode_imag = jnp.einsum("fbx,fbm->fmx", part_real, coef_imag, precision=HIGH) + jnp.einsum(
        "fbx,fbm->fmx", part_imag, coef_real, precision=HIGH
    )
    modes = jnp.stack([mode_real, mode_imag], axis=2).reshape(local_freqs, nblocks, 2, nvars, npts)
    spectrum = nfreq * nblocks * eigen / total
    return (modes, spectrum)


def solution(mesh):
    return jax.shard_map(
        body,
        mesh=mesh,
        in_specs=(P("blk", None, "pts"), P(None, "pts"), P(), P()),
        out_specs=(P("blk", None, None, None, "pts"), P("blk", None)),
        check_vma=False,
    )
```

profile of v0, /device:TPU:1, one launch (start us, length us, event | category | flops | bytes accessed | tf_op | source)
XLA Modules:
  0.0 1354.6 jit_solution(2946811667927252109)
XLA Ops:
  0.6 1.3 copy.67
  2.0 8.8 collective-permute-start
  17.3 0.9 copy.69
  18.2 10.2 all-to-all-start
  28.5 14.1 %all-to-all-done = f32[64,1,2,5,128]{4,2,3,1,0:T(2,128)S(1)} async-done(((f32[64,1,2,5,128]{4,2,3,1,0:T(2,128)}), f32[64,1,2,5,128]{4,2,3,1,0:T(2,128)S(1)}, u32[]{:S(2)}, u32[]{:S(2)}) %all-to-all-start) | async-done | bytes 327712 | tf_op jit(solution)/shard_map/all_to_all | solution.py:119
  44.6 29.3 %all-reduce = (f32[1,64,64]{2,1,0:T(8,128)S(1)}, f32[1,64,64]{2,1,0:T(8,128)S(1)}) all-reduce(f32[1,64,64]{2,1,0:T(8,128)S(1)} %fusion.12, f32[1,64,64]{2,1,0:T(8,128)S(1)} %fusion.15), channel_id=1, replica_groups=mesh['blk'=64,'pts'=8] {'pts'}, use_global_device_ids=true, to_apply=%region_0.1 | all-reduce | flops 8192 | bytes 65536 | tf_op jit(solution)/shard_map/psum | solution.py:134
  74.1 1143.6 %while.20 = (s32[]{:T(128)}, f32[1,64,64]{1,2,0:T(8,128)S(1)}, f32[1,64,64]{1,2,0:T(8,128)S(1)}, f32[1,64,64]{1,2,0:T(8,128)S(1)}, f32[1,64,64]{1,2,0:T(8,128)S(...) while((s32[]{:T(128)}, f32[1,64,64]{1,2,0:T(8,128)S(1)}, f32[1,64,64]{1,2,0:T(8,128)S(1)}, ...), condition=%wide.region_3.8_spmd.clone, body=%wide.region_2.7_spmd.clone.sunk | while | flops 165962 | bytes 674198 | solution.py:86
  74.1 0.8 gather_fusion.4
  75.8 0.8 gather_fusion.3
  83.2 0.8 gather_fusion.4
  84.8 0.8 gather_fusion.3
  92.3 0.8 gather_fusion.4
  93.9 0.8 gather_fusion.3
  101.4 0.8 gather_fusion.4
  103.0 0.8 gather_fusion.3
  110.4 0.8 gather_fusion.4
  121.2 0.8 gather_fusion.3
  128.6 0.8 gather_fusion.4
  130.2 0.8 gather_fusion.3
  137.7 0.8 gather_fusion.4
  139.3 0.8 gather_fusion.3
  148.4 0.8 gather_fusion.3
  155.8 0.8 gather_fusion.4
  157.5 0.8 gather_fusion.3
  164.9 0.8 gather_fusion.4
  174.0 0.8 gather_fusion.4
  175.6 0.8 gather_fusion.3
  184.7 0.8 gather_fusion.3
  192.1 0.8 gather_fusion.4
  193.8 0.8 gather_fusion.3
  201.2 0.8 gather_fusion.4
  210.3 0.8 gather_fusion.4
  219.3 0.8 gather_fusion.4
  221.0 0.8 gather_fusion.3
  228.4 0.8 gather_fusion.4
  237.5 0.8 gather_fusion.4
  246.6 0.8 gather_fusion.4
  255.6 0.8 gather_fusion.4
  257.3 0.8 gather_fusion.3
  264.7 0.8 gather_fusion.4
  266.4 0.8 gather_fusion.3
  273.8 0.8 gather_fusion.4
  275.4 0.8 gather_fusion.3
  282.9 0.8 gather_fusion.4
  284.5 0.8 gather_fusion.3
  292.0 0.8 gather_fusion.4
  302.7 0.8 gather_fusion.3
  310.1 0.8 gather_fusion.4
  320.8 0.8 gather_fusion.3
  329.9 0.8 gather_fusion.3
  339.0 0.8 gather_fusion.3
  346.4 0.8 gather_fusion.4
  348.1 0.8 gather_fusion.3
  355.5 0.8 gather_fusion.4
  357.1 0.8 gather_fusion.3
  366.2 0.8 gather_fusion.3
  373.6 0.8 gather_fusion.4
  384.4 0.8 gather_fusion.3
  391.8 0.8 gather_fusion.4
  400.9 0.8 gather_fusion.4
  411.6 0.8 gather_fusion.3
  1219.1 131.3 %psum.23 = f32[]{:T(128)} all-reduce(f32[]{:T(128)} %reduce_sum.29), channel_id=1, replica_groups=mesh['blk'=64,'pts'=8] {'blk'}, use_global_device_ids=true, to_apply=%region_7.12 | all-reduce | flops 1 | bytes 8 | tf_op jit(solution)/shard_map/psum | solution.py:137
  1350.6 1.2 fusion.64
  1353.6 1.0 copy.75
  (3646 shorter events, 1098.5 us)
Async XLA Ops:
  2.0 14.6 %collective-permute-start = (f32[256,640]{0,1:T(8,128)S(1)}, f32[256,640]{0,1:T(8,128)S(1)}, u32[]{:S(2)}, u32[]{:S(2)}) collective-permute-start(f32[256,640]{0,1:T(8,128)S(1)} %bitcast.329), channel_id=1, source_target_pairs={{8,0},{16,8},{24,16},{32,24},{40,32},{48,40},{56,48},{64,56},{72,6... | collective-permute-start | bytes 1966088 | tf_op jit(solution)/shard_map/ppermute | solution.py:18
  10.8 0.7 copy-start.2
  14.1 0.7 copy-start.1
  18.2 24.4 %all-to-all-start = ((f32[64,1,2,5,128]{4,2,3,1,0:T(2,128)}), f32[64,1,2,5,128]{4,2,3,1,0:T(2,128)S(1)}, u32[]{:S(2)}, u32[]{:S(2)}) async-start(f32[64,1,2,5,128]{4,2,3,1,0:T(2,128)} %copy.69), calls=%async_computation | async-start | bytes 655360 | tf_op jit(solution)/shard_map/all_to_all | solution.py:119
  42.6 0.7 copy-start
where the time goes:
time: 1350 us
  local copies, waits for them, and re-layouts  1100 us (81%)
  blocking collectives  161 us (12%)
  other arithmetic  41.8 us (3%)
  starting transfers between devices  19 us (1%)
  waiting for transfers between devices  14.1 us (1%)
    gather x252, local copies, waits for them, and re-layouts, right_apply(): swap_imag = jnp.take(left_imag, partner, axis=-1)  150 us
    gather x252, local copies, waits for them, and re-layouts, right_apply(): swap_real = jnp.take(left_real, partner, axis=-1)  150 us
    psum x1, blocking collectives, body(): total = lax.psum(jnp.sum(eigen), 'blk')  131 us
    gather x126, local copies, waits for them, and re-layouts, rotate_round(): pair_real = jnp.take_along_axis(real_a, columns, axis=-1)[..., 0]  102 us
    gather x126, local copies, waits for them, and re-layouts, rotate_round(): diagonal = jnp.diagonal(real_a, axis1=-2, axis2=-1)  102 us
    gather x126, local copies, waits for them, and re-layouts, rotate_round(): pair_imag = jnp.take_along_axis(imag_a, columns, axis=-1)[..., 0]  102 us
    gather x126, local copies, waits for them, and re-layouts, rotate_round(): moved_imag = jnp.take(off_imag, partner, axis=-1)  99.6 us
    gather x126, local copies, waits for them, and re-layouts, rotate_round(): moved_real = jnp.take(off_real, partner, axis=-1)  98.1 us
  transfers between devices with their start and end apart: 2, of which 1 were waited for; matrix products, arithmetic and copies ran while one was open for 0% of the time, Pallas kernels for 0%

commit v1 on v0

v1 whole, which is shorter than its diff:
```python
import functools
import math

import jax
import jax.numpy as jnp
from jax import lax
from jax.experimental import pallas as pl
from jax.experimental.pallas import tpu as pltpu
from jax.sharding import PartitionSpec as P

SWEEPS = 2
HIGH = lax.Precision.HIGHEST
DAMPING = 0.01
F32 = jnp.float32
NFFT = 256
NB = 64
LANES = 128
GROUPS = 4
UNROLL = 7
PARAMS = pltpu.CompilerParams(vmem_limit_bytes=16 << 20)


def table_kernel(block_ref, offsets_ref, freqs_ref, table_ref):
    offset = offsets_ref[block_ref[0]]
    lag = jnp.bitwise_and(lax.broadcasted_iota(jnp.int32, (1, NFFT), 1) - offset, NFFT - 1)
    unit = 2.0 * math.pi / NFFT
    hann = (0.5 - 0.5 * jnp.cos(unit * lag.astype(F32))) / math.sqrt(NFFT)
    phase = jnp.bitwise_and(freqs_ref[...] * lag, NFFT - 1)
    angle = unit * phase.astype(F32)
    table_ref[:NB, :] = hann * jnp.cos(angle)
    table_ref[NB:, :] = -hann * jnp.sin(angle)


def spectra_kernel(scale, block_ref, offsets_ref, table_ref, own_ref, next_ref, weights_ref, out_ref, energy_ref):
    offset = offsets_ref[block_ref[0]]
    mine = lax.broadcasted_iota(jnp.int32, (NFFT, LANES), 0) >= offset
    nvars = own_ref.shape[0]
    energy = jnp.zeros((8, LANES), F32)
    for v in range(nvars):
        data = jnp.where(mine, own_ref[v], next_ref[v])
        result = jnp.dot(table_ref[...], data, precision=HIGH, preferred_element_type=F32)
        for part in range(2):
            out_ref[pl.ds(2 * v + part, NB, stride=2 * nvars), :] = result[part * NB : (part + 1) * NB]
        square = jnp.sum((result * result).reshape(-1, 8, LANES), axis=0)
        energy = energy + square * (weights_ref[v : v + 1, :] * scale)
    energy_ref[...] = energy


def gram_kernel(scale, q_ref, weights_ref, gram_ref):
    nvars = weights_ref.shape[0]
    left, right_real, right_imag = [], [], []
    for v in range(nvars):
        real = q_ref[pl.ds(2 * v, NB, stride=2 * nvars), :]
        imag = q_ref[pl.ds(2 * v + 1, NB, stride=2 * nvars), :]
        weight = weights_ref[v : v + 1, :] * scale
        left += [real * weight, imag * weight]
        right_real += [real, imag]
        right_imag += [imag, -real]
    right = jnp.concatenate([jnp.concatenate(right_real, 1), jnp.concatenate(right_imag, 1)], 0)
    gram_ref[...] = lax.dot_general(
        jnp.concatenate(left, 1), right, (((1,), (1,)), ((), ())), precision=HIGH, preferred_element_type=F32
    )


def rotate(state, offset, ranks):
    top, bottom, diag_t, diag_b = state
    new_top, new_bottom, new_dt, new_db = [], [], [], []
    for v in range(GROUPS):
        zt, izt, xt, ixt = top[v]
        zb, izb, xb, ixb = bottom[v]
        real = jnp.sum(zt * xb, axis=1, keepdims=True)
        imag = jnp.sum(zt * ixb, axis=1, keepdims=True)
        at, ab = diag_t[v], diag_b[v]
        sign = jnp.where(ranks[v] > offset, 1.0, -1.0)
        delta = sign * (ab - at)
        four = 4.0 * (real * real + imag * imag)
        square = delta * delta + four
        radius = square * lax.rsqrt(jnp.maximum(square, 1e-37))
        upper = radius + delta + DAMPING * (ab + at)
        inverse = lax.rsqrt(upper * upper + four)
        cosine = upper * inverse
        twice = (sign + sign) * inverse
        off_r, off_i = twice * real, twice * imag
        cc = cosine * cosine
        oo = off_r * off_r + off_i * off_i
        cross = (cosine + cosine) * (off_r * real + off_i * imag)
        new_dt.append(cc * at + oo * ab - cross)
        new_db.append(cc * ab + oo * at + cross)
        new_top.append(
            (
                cosine * zt - off_r * zb - off_i * izb,
                cosine * izt - off_r * izb + off_i * zb,
                cosine * xt - off_r * xb - off_i * ixb,
                cosine * ixt - off_r * ixb + off_i * xb,
            )
        )
        new_bottom.append(
            (
                cosine * zb + off_r * zt - off_i * izt,
                cosine * izb + off_r * izt + off_i * zt,
                cosine * xb + off_r * xt - off_i * ixt,
                cosine * ixb + off_r * ixt + off_i * xt,
            )
        )
    return new_top, new_bottom, new_dt, new_db


def advance(state):
    top, bottom, diag_t, diag_b = state
    row = lax.broadcasted_iota(jnp.int32, (8, LANES), 0)

    def ring(tops, bottoms):
        last = jnp.where(row == 7, bottoms[3], pltpu.roll(tops[0], 7, 0))
        first = jnp.where(row == 0, bottoms[0], pltpu.roll(bottoms[3], 1, 0))
        second = jnp.where(row == 0, tops[0], bottoms[0])
        return [tops[1], tops[2], tops[3], last], [first, second, bottoms[1], bottoms[2]]

    parts = [ring([t[i] for t in top], [b[i] for b in bottom]) for i in range(4)]
    new_top = [tuple(parts[i][0][v] for i in range(4)) for v in range(GROUPS)]
    new_bottom = [tuple(parts[i][1][v] for i in range(4)) for v in range(GROUPS)]
    new_dt, new_db = ring(diag_t, diag_b)
    return new_top, new_bottom, new_dt, new_db


def modes_kernel(gram_ref, q_ref, lam_ref, modes_ref, rows_ref):
    lane = lax.broadcasted_iota(jnp.int32, (8, LANES), 1)
    sub = lax.broadcasted_iota(jnp.int32, (8, LANES), 0)
    for v in range(GROUPS):
        for s in range(8):
            p = GROUPS * s + v
            rows_ref[8 * v + s : 8 * v + s + 1, :] = gram_ref[p : p + 1, :]
            rows_ref[32 + 8 * v + s : 33 + 8 * v + s, :] = gram_ref[63 - p : 64 - p, :]
    flip = jnp.where(lane < NB, -1.0, 1.0)
    top, bottom, diag_t, diag_b, ranks = [], [], [], [], []
    for v in range(GROUPS):
        p = GROUPS * sub + v
        for base, index, rows, diag in ((0, p, top, diag_t), (32, 63 - p, bottom, diag_b)):
            z = rows_ref[base + 8 * v : base + 8 * v + 8, :]
            x = jnp.where(lane == index, 1.0, 0.0)
            ix = jnp.where(lane == index + NB, 1.0, 0.0)
            rows.append((z, flip * pltpu.roll(z, NB, 1), x, ix))
            diag.append(jnp.broadcast_to(jnp.sum(z * x, axis=1, keepdims=True), (8, LANES)))
        ranks.append(jnp.where(p == 0, 1000, p))
    flat, tree = jax.tree.flatten((top, bottom, diag_t, diag_b))

    def some_rounds(step, flat):
        state = jax.tree.unflatten(tree, flat)
        base = lax.rem(step * UNROLL, NB - 1)
        for i in range(UNROLL):
            offset = 31 - jnp.abs(base + i - 31)
            state = advance(rotate(state, offset, ranks))
        return jax.tree.flatten(state)[0]

    flat = lax.fori_loop(0, SWEEPS * (NB - 1) // UNROLL, some_rounds, flat)
    top, bottom, diag_t, diag_b = jax.tree.unflatten(tree, flat)
    for v in range(GROUPS):
        for rows, diag, low in ((top[v], diag_t[v], True), (bottom[v], diag_b[v], False)):
            x, ix = rows[2], rows[3]
            left = lane < NB
            sum_real = jnp.sum(jnp.where(left, x, 0.0), axis=1, keepdims=True)
            sum_imag = -jnp.sum(jnp.where(left, 0.0, x), axis=1, keepdims=True)
            magnitude = jnp.sqrt(sum_real * sum_real + sum_imag * sum_imag)
            scaling = 1.0 / (jnp.maximum(magnitude, 1.0) * jnp.sqrt(NB * (diag + 1e-06)))
            phase_r, phase_i = sum_real * scaling, -sum_imag * scaling
            coef = jnp.where(left, 1.0, -1.0) * (x * phase_r - ix * phase_i)
            for s in range(8):
                p = GROUPS * s + v
                row = p if low else 63 - p
                rows_ref[row : row + 1, :] = coef[s : s + 1, :]
                lam_ref[row : row + 1, :] = diag[s : s + 1, :]
    nparts = q_ref.shape[0] // NB
    coefs = rows_ref[...]
    lhs = jnp.concatenate([coefs[:, :NB], coefs[:, NB:]], 0)
    for v in range(nparts // 2):
        real = q_ref[pl.ds(2 * v, NB, stride=nparts), :]
        imag = q_ref[pl.ds(2 * v + 1, NB, stride=nparts), :]
        out = jnp.dot(lhs, jnp.concatenate([real, imag], 1), precision=HIGH, preferred_element_type=F32)
        modes_ref[pl.ds(2 * v, NB, stride=nparts), :] = out[:NB, :LANES] - out[NB:, LANES:]
        modes_ref[pl.ds(2 * v + 1, NB, stride=nparts), :] = out[:NB, LANES:] + out[NB:, :LANES]


def spec(space):
    return pl.BlockSpec(memory_space=space)


def summed(part, axis):
    size = lax.axis_size(axis)
    step = 1
    while step < size:
        part = part + lax.ppermute(part, axis, [(i, i ^ step) for i in range(size)])
        step *= 2
    return part


def body(snapshots, weights, offsets, freqs):
    nfft, nvars, npts = snapshots.shape
    nfreq = freqs.shape[0]
    nblocks = lax.axis_size("blk")
    total_pts = npts * lax.axis_size("pts")
    block = lax.axis_index("blk").astype(jnp.int32).reshape(1)
    own = jnp.transpose(snapshots, (1, 0, 2))
    route = [(i + 1, i) for i in range(nblocks - 1)]
    following = lax.ppermute(own, "blk", route)
    table = pl.pallas_call(
        table_kernel,
        out_shape=jax.ShapeDtypeStruct((2 * nfreq, nfft), F32),
        in_specs=[spec(pltpu.SMEM), spec(pltpu.SMEM), spec(pltpu.VMEM)],
        compiler_params=PARAMS,
        name="table",
    )(block, offsets, freqs.reshape(nfreq, 1))
    scale = 1.0 / (nblocks * nvars * total_pts)
    spectra, energy = pl.pallas_call(
        functools.partial(spectra_kernel, scale),
        out_shape=[
            jax.ShapeDtypeStruct((nfreq * 2 * nvars, npts), F32),
            jax.ShapeDtypeStruct((8, npts), F32),
        ],
        in_specs=[spec(pltpu.SMEM), spec(pltpu.SMEM)] + [spec(pltpu.VMEM)] * 4,
        compiler_params=PARAMS,
        name="spectra",
    )(block, offsets, table, own, following, weights)
    energies = lax.all_gather(energy, ("blk", "pts"), axis=0, tiled=True)
    grouped = lax.all_to_all(
        spectra.reshape(nfreq, 1, nvars, 2, npts), "blk", split_axis=0, concat_axis=1, tiled=True
    ).reshape(nblocks * 2 * nvars, npts)
    gram = pl.pallas_call(
        functools.partial(gram_kernel, scale),
        out_shape=jax.ShapeDtypeStruct((nblocks, 2 * nblocks), F32),
        compiler_params=PARAMS,
        name="gram",
    )(grouped, weights)
    gram = summed(gram, "pts")
    lam, modes = pl.pallas_call(
        modes_kernel,
        out_shape=[
            jax.ShapeDtypeStruct((nblocks, LANES), F32),
            jax.ShapeDtypeStruct((nblocks * 2 * nvars, npts), F32),
        ],
        scratch_shapes=[pltpu.VMEM((nblocks, LANES), F32)],
        compiler_params=PARAMS,
        name="modes",
    )(gram, grouped)
    eigen = lam[:, 0].reshape(1, nblocks)
    total = jnp.sum(energies)
    modes = modes.reshape(1, nblocks, nvars, 2, npts).transpose(0, 1, 3, 2, 4)
    return modes, nfreq * nblocks * eigen / total


def solution(mesh):
    return jax.shard_map(
        body,
        mesh=mesh,
        in_specs=(P("blk", None, "pts"), P(None, "pts"), P(), P()),
        out_specs=(P("blk", None, None, None, "pts"), P("blk", None)),
        check_vma=False,
    )
```

time: 1350 us -> 158 us (0.12)
  local copies, waits for them, and re-layouts: 1100 us -> 3.83 us
  blocking collectives: 161 us -> 26 us
  waiting for transfers between devices: 14.1 us -> 61.5 us
  other arithmetic: 41.8 us -> 4.08 us
  Pallas kernels: 0 us -> 20.8 us
    gather x1765 -> x0, local copies, waits for them, and re-layouts: 1070 us -> none  [the longest x252 150 us: right_apply(): swap_imag = jnp.take(left_imag, partner, axis=-1)]
    psum x2 -> x0, blocking collectives: 161 us -> none  [the longest x1 131 us: body(): total = lax.psum(jnp.sum(eigen), 'blk')]
    all_gather x0 -> x1, waiting for transfers between devices: none -> 55.2 us  [body(): energies = lax.all_gather(energy, ('blk', 'pts'), axis=0, tiled=True)]
    all_to_all x0 -> x1, blocking collectives: none -> 26 us  [body(): lax.all_to_all(spectra.reshape(nfreq, 1, nvars, 2, npts), 'blk', split_ax...]
    pallas_call x0 -> x4, Pallas kernels: none -> 20.8 us  [the longest x1 17.3 us: body(): pl.pallas_call(modes_kernel, out_shape=[jax.ShapeDtypeStruct((nblocks, LA...]
    another operation x384 -> x0, local copies, waits for them, and re-layouts: 20.5 us -> none  [the longest x126 9.48 us: rotate_round(): swap_real = jnp.take(half_real, partner, axis=-2)]
    ppermute x1 -> x4, starting transfers between devices: 8.79 us -> 26.9 us  [the longest x3 18.1 us: summed(): part = part + lax.ppermute(part, axis, [(i, i ^ step) for i in range(size)])]
    all_to_all x1 -> x0, waiting for transfers between devices: 14.1 us -> none  [body(): lax.all_to_all(spectra[:, None], 'blk', split_axis=0, concat_axis=1, tile...]
  transfers between devices with their start and end apart: 2 -> 5, of which waited for: 1 -> 5; matrix products, arithmetic and copies ran while one was open for 0% -> 0% of each run, Pallas kernels for 0% -> 12%
where the time goes in v1:
time: 158 us; the launch traced here: 157 us
  waiting for transfers between devices  61.5 us (39%)
  starting transfers between devices  27 us (17%)
  blocking collectives  26 us (16%)
  Pallas kernels  20.8 us (13%)
  between operations  14.1 us (9%)
  other arithmetic  4.08 us (3%)
  local copies, waits for them, and re-layouts  3.83 us (2%)
    all_gather x1, waiting for transfers between devices, body(): energies = lax.all_gather(energy, ('blk', 'pts'), axis=0, tiled=True)  55.2 us
    all_to_all x1, blocking collectives, body(): lax.all_to_all(spectra.reshape(nfreq, 1, nvars, 2, npts), 'blk', split_ax...  26 us
    ppermute x3, starting transfers between devices, summed(): part = part + lax.ppermute(part, axis, [(i, i ^ step) for i in range(size)])  18.1 us
    pallas_call x1, Pallas kernels, body(): pl.pallas_call(modes_kernel, out_shape=[jax.ShapeDtypeStruct((nblocks, LA...  17.3 us
    ppermute x1, starting transfers between devices, body(): following = lax.ppermute(own, 'blk', route)  8.79 us
    ppermute x3, waiting for transfers between devices, summed(): part = part + lax.ppermute(part, axis, [(i, i ^ step) for i in range(size)])  4.38 us
  transfers between devices with their start and end apart: 5, of which 5 were waited for; matrix products, arithmetic and copies ran while one was open for 0% of the time, Pallas kernels for 12%

profile of v1, /device:TPU:1, one launch (start us, length us, event | category | flops | bytes accessed | tf_op | source)
XLA Modules:
  0.0 157.3 jit_solution(6378710444202699843)
XLA Ops:
  7.2 0.0 copy-start.2
  7.2 0.0 all-gather.2.cloned.1.call-start
  7.2 8.8 %collective-permute-start = (f32[5,256,128]{2,1,0:T(8,128)}, f32[5,256,128]{2,1,0:T(8,128)S(1)}, u32[]{:S(2)}, u32[]{:S(2)}) collective-permute-start(f32[5,256,128]{2,1,0:T(8,128)} %bitcast.13), channel_id=1, source_target_pairs={{8,0},{16,8},{24,16},{32,24},{40,32},{48,40},{56,48},{64,56},{72,6... | collective-permute-start | bytes 1966088 | tf_op jit(solution)/shard_map/ppermute | solution.py:203
  16.0 0.7 copy.8.freqs_ref
  16.8 0.0 copy-start.3
  16.8 0.7 copy-done.3
  17.4 0.9 table.1.table_ref
  18.3 1.9 %collective-permute-done.next_ref = f32[5,256,128]{2,1,0:T(8,128)S(1)} collective-permute-done((f32[5,256,128]{2,1,0:T(8,128)}, f32[5,256,128]{2,1,0:T(8,128)S(1)}, u32[]{:S(2)}, u32[]{:S(2)}) %collective-permute-start) | collective-permute-done | bytes 655392 | tf_op jit(solution)/shard_map/ppermute | solution.py:203
  20.2 0.0 copy-start
  20.2 1.1 copy-done
  21.3 0.0 copy-start.1
  21.3 0.7 copy-done.1
  22.0 0.0 copy-start.4
  22.0 0.7 copy-done.4
  22.6 1.9 %spectra.1 = (f32[640,128]{1,0:T(8,128)S(1)}, f32[8,128]{1,0:T(8,128)}) custom-call(s32[1]{0:T(128)} %bitcast.block_ref, s32[64]{0:T(128)S(1)} %copy-done.4, f32[128,256]{1,0:T(8,128)S(1)} %table.1.table_ref, f32[5,256,128]{2,1,0:T(8,128)S(1)} %bitcast.14, f32[5,256,128]{2,1,0:T(8,128)S(1)} %collective-permute-done.next_ref, f32[5,128]{1,0:T(8,128)S(1)} %copy-done.1), custom_call_target="tpu_custom_call" | custom-call | tf_op jit(solution)/shard_map/spectra/pallas_call | solution.py:212
  24.5 0.0 all-gather.2.cloned.1.call-update
  24.6 26.0 %all_to_all.4 = f32[64,1,5,2,128]{4,3,2,1,0:T(2,128)S(1)} all-to-all(f32[64,1,5,2,128]{4,3,2,1,0:T(2,128)S(1)} %bitcast.15), channel_id=1, replica_groups=mesh['blk'=64,'pts'=8] {'blk'}, dimensions={0} | all-to-all | bytes 655360 | tf_op jit(solution)/shard_map/all_to_all | solution.py:223
  50.6 0.0 copy-done.2
  50.6 0.8 gram.1
  51.4 4.0 %collective-permute-start.1 = (f32[64,128]{1,0:T(8,128)S(1)}, f32[64,128]{1,0:T(8,128)S(1)}, u32[]{:S(2)}, u32[]{:S(2)}) collective-permute-start(f32[64,128]{1,0:T(8,128)S(1)} %gram.1), channel_id=1, source_target_pairs={{0,1},{1,0},{2,3},{3,2},{4,5},{5,4},{6,7},{7,6},{8,9},{9,8},{10,11... | collective-permute-start | bytes 98312 | tf_op jit(solution)/shard_map/ppermute | solution.py:190
  55.4 1.6 %collective-permute-done.1 = f32[64,128]{1,0:T(8,128)S(1)} collective-permute-done((f32[64,128]{1,0:T(8,128)S(1)}, f32[64,128]{1,0:T(8,128)S(1)}, u32[]{:S(2)}, u32[]{:S(2)}) %collective-permute-start.1) | collective-permute-done | bytes 32800 | tf_op jit(solution)/shard_map/ppermute | solution.py:190
  57.0 5.9 %collective-permute-start.2 = (f32[64,128]{1,0:T(8,128)S(1)}, f32[64,128]{1,0:T(8,128)S(1)}, u32[]{:S(2)}, u32[]{:S(2)}) collective-permute-start(f32[64,128]{1,0:T(8,128)S(1)} %add.9), channel_id=1, source_target_pairs={{0,2},{1,3},{2,0},{3,1},{4,6},{5,7},{6,4},{7,5},{8,10},{9,11},{10,... | collective-permute-start | bytes 98312 | tf_op jit(solution)/shard_map/ppermute | solution.py:190
  62.9 1.5 collective-permute-done.2
  64.4 8.2 %collective-permute-start.3 = (f32[64,128]{1,0:T(8,128)S(1)}, f32[64,128]{1,0:T(8,128)S(1)}, u32[]{:S(2)}, u32[]{:S(2)}) collective-permute-start(f32[64,128]{1,0:T(8,128)S(1)} %add.10), channel_id=1, source_target_pairs={{0,4},{1,5},{2,6},{3,7},{4,0},{5,1},{6,2},{7,3},{8,12},{9,13},{10,... | collective-permute-start | bytes 98312 | tf_op jit(solution)/shard_map/ppermute | solution.py:190
  72.6 1.3 collective-permute-done.3
  73.9 17.3 %modes.1 = (f32[64,128]{1,0:T(8,128)S(1)}, f32[640,128]{1,0:T(8,128)}) custom-call(f32[64,128]{1,0:T(8,128)S(1)} %add.11.gram_ref, f32[640,128]{1,0:T(8,128)S(1)} %bitcast.12), custom_call_target="tpu_custom_call" | custom-call | tf_op jit(solution)/shard_map/modes/pallas_call | solution.py:233
  91.2 55.2 %all-gather.2.cloned.1.call-done = f32[4096,128]{1,0:T(8,128)} async-done(((f32[8,128]{1,0:T(8,128)}), f32[4096,128]{1,0:T(8,128)}) %all-gather.2.cloned.1.call-update) | async-done | bytes 2097168 | tf_op jit(solution)/shard_map/all_gather | solution.py:222
  146.4 2.8 %reduce_sum.9 = f32[]{:T(128)} reduce(f32[4096,128]{1,0:T(8,128)} %all-gather.2.cloned.1.call-done, f32[]{:T(128)} %constant.9.clone.1), dimensions={0,1}, to_apply=%region_0.0 | reduce | flops 524287 | bytes 2097160 | tf_op jit(solution)/shard_map/reduce_sum | solution.py:244
  149.2 1.3 fusion
  (3 shorter events, 0.0 us)
Async XLA Ops:
  7.2 43.4 %copy-start.2 = (f32[5,128]{1,0:T(8,128)S(1)}, f32[5,128]{1,0:T(8,128)}, u32[]{:S(2)}) copy-start(f32[5,128]{1,0:T(8,128)} %weights_ref.3) | copy-start | bytes 7684
  7.2 139.2 %all-gather.2.cloned.1.call-start = ((), (), s32[]{:S(2)}) async-start(), calls=%async_computation.1 | async-start | bytes 2101248 | tf_op jit(solution)/shard_map/all_gather | solution.py:222
  7.2 13.0 %collective-permute-start = (f32[5,256,128]{2,1,0:T(8,128)}, f32[5,256,128]{2,1,0:T(8,128)S(1)}, u32[]{:S(2)}, u32[]{:S(2)}) collective-permute-start(f32[5,256,128]{2,1,0:T(8,128)} %bitcast.13), channel_id=1, source_target_pairs={{8,0},{16,8},{24,16},{32,24},{40,32},{48,40},{56,48},{64,56},{72,6... | collective-permute-start | bytes 1966088 | tf_op jit(solution)/shard_map/ppermute | solution.py:203
  16.8 0.7 copy-start.3
  20.2 1.1 copy-start
  21.3 0.7 copy-start.1
  22.0 0.7 copy-start.4
  51.4 5.6 %collective-permute-start.1 = (f32[64,128]{1,0:T(8,128)S(1)}, f32[64,128]{1,0:T(8,128)S(1)}, u32[]{:S(2)}, u32[]{:S(2)}) collective-permute-start(f32[64,128]{1,0:T(8,128)S(1)} %gram.1), channel_id=1, source_target_pairs={{0,1},{1,0},{2,3},{3,2},{4,5},{5,4},{6,7},{7,6},{8,9},{9,8},{10,11... | collective-permute-start | bytes 98312 | tf_op jit(solution)/shard_map/ppermute | solution.py:190
  57.0 7.4 %collective-permute-start.2 = (f32[64,128]{1,0:T(8,128)S(1)}, f32[64,128]{1,0:T(8,128)S(1)}, u32[]{:S(2)}, u32[]{:S(2)}) collective-permute-start(f32[64,128]{1,0:T(8,128)S(1)} %add.9), channel_id=1, source_target_pairs={{0,2},{1,3},{2,0},{3,1},{4,6},{5,7},{6,4},{7,5},{8,10},{9,11},{10,... | collective-permute-start | bytes 98312 | tf_op jit(solution)/shard_map/ppermute | solution.py:190
  64.4 9.5 %collective-permute-start.3 = (f32[64,128]{1,0:T(8,128)S(1)}, f32[64,128]{1,0:T(8,128)S(1)}, u32[]{:S(2)}, u32[]{:S(2)}) collective-permute-start(f32[64,128]{1,0:T(8,128)S(1)} %add.10), channel_id=1, source_target_pairs={{0,4},{1,5},{2,6},{3,7},{4,0},{5,1},{6,2},{7,3},{8,12},{9,13},{10,... | collective-permute-start | bytes 98312 | tf_op jit(solution)/shard_map/ppermute | solution.py:190
Sparse Core Ops, SparseCore 0:
  24.7 121.6 all-gather.1

commit v2 on v1

--- a/solution.py
+++ b/solution.py
@@ -20,46 +20,79 @@
 PARAMS = pltpu.CompilerParams(vmem_limit_bytes=16 << 20)
 
 
-def table_kernel(block_ref, offsets_ref, freqs_ref, table_ref):
-    offset = offsets_ref[block_ref[0]]
-    lag = jnp.bitwise_and(lax.broadcasted_iota(jnp.int32, (1, NFFT), 1) - offset, NFFT - 1)
+def half_spectra_kernel(tail, nvars, place_ref, offsets_ref, freqs_ref, own_ref, out_ref, data_ref, sem):
+    copies = [pltpu.make_async_copy(own_ref.at[v], data_ref.at[v], sem.at[v]) for v in range(nvars)]
+    for copy in copies:
+        copy.start()
+    block = place_ref[0]
+    offset = offsets_ref[jnp.maximum(block - 1, 0) if tail else block]
+    snapshot = lax.broadcasted_iota(jnp.int32, (1, NFFT), 1)
+    lag = jnp.bitwise_and(snapshot - offset, NFFT - 1)
+    valid = snapshot < offset if tail else snapshot >= offset
     unit = 2.0 * math.pi / NFFT
-    hann = (0.5 - 0.5 * jnp.cos(unit * lag.astype(F32))) / math.sqrt(NFFT)
-    phase = jnp.bitwise_and(freqs_ref[...] * lag, NFFT - 1)
-    angle = unit * phase.astype(F32)
-    table_ref[:NB, :] = hann * jnp.cos(angle)
-    table_ref[NB:, :] = -hann * jnp.sin(angle)
-
-
-def spectra_kernel(scale, block_ref, offsets_ref, table_ref, own_ref, next_ref, weights_ref, out_ref, energy_ref):
-    offset = offsets_ref[block_ref[0]]
-    mine = lax.broadcasted_iota(jnp.int32, (NFFT, LANES), 0) >= offset
-    nvars = own_ref.shape[0]
-    energy = jnp.zeros((8, LANES), F32)
+    hann = jnp.where(valid, 0.5 - 0.5 * jnp.cos(unit * lag.astype(F32)), 0.0) / math.sqrt(NFFT)
+    square = (NB, NB)
+    same = lax.broadcasted_iota(jnp.int32, square, 0) == lax.broadcasted_iota(jnp.int32, square, 1)
+    freqs = jnp.sum(jnp.where(same, freqs_ref[...].astype(F32), 0.0), axis=1, keepdims=True).astype(jnp.int32)
+    angle = unit * jnp.bitwise_and(freqs * lag, NFFT - 1).astype(F32)
+    table = jnp.concatenate([hann * jnp.cos(angle), -hann * jnp.sin(angle)], 0)
     for v in range(nvars):
-        data = jnp.where(mine, own_ref[v], next_ref[v])
-        result = jnp.dot(table_ref[...], data, precision=HIGH, preferred_element_type=F32)
+        copies[v].wait()
+        result = jnp.dot(table, data_ref[v], precision=HIGH, preferred_element_type=F32)
         for part in range(2):
             out_ref[pl.ds(2 * v + part, NB, stride=2 * nvars), :] = result[part * NB : (part + 1) * NB]
-        square = jnp.sum((result * result).reshape(-1, 8, LANES), axis=0)
-        energy = energy + square * (weights_ref[v : v + 1, :] * scale)
-    energy_ref[...] = energy
-
-
-def gram_kernel(scale, q_ref, weights_ref, gram_ref):
+
+
+def join_kernel(scale, head_ref, tail_ref, weights_ref, out_ref):
     nvars = weights_ref.shape[0]
+    rows = 2 * nvars + 1
+    energy = jnp.zeros((1, LANES), F32)
+    for j in range(2 * nvars):
+        value = head_ref[pl.ds(j, NB, stride=2 * nvars), :] + tail_ref[pl.ds(j, NB, stride=2 * nvars), :]
+        out_ref[pl.ds(j, NB, stride=rows), :] = value
+        weight = weights_ref[j // 2 : j // 2 + 1, :] * scale
+        energy = energy + jnp.sum(value * value, axis=0, keepdims=True) * weight
+    out_ref[pl.ds(rows - 1, NB, stride=rows), :] = jnp.broadcast_to(energy, (NB, LANES))
+
+
+def gram_kernel(scale, copies, q_ref, weights_ref, out_ref):
+    nvars = weights_ref.shape[0]
+    rows = 2 * nvars + 1
     left, right_real, right_imag = [], [], []
     for v in range(nvars):
-        real = q_ref[pl.ds(2 * v, NB, stride=2 * nvars), :]
-        imag = q_ref[pl.ds(2 * v + 1, NB, stride=2 * nvars), :]
+        real = q_ref[pl.ds(2 * v, NB, stride=rows), :]
+        imag = q_ref[pl.ds(2 * v + 1, NB, stride=rows), :]
         weight = weights_ref[v : v + 1, :] * scale
         left += [real * weight, imag * weight]
         right_real += [real, imag]
         right_imag += [imag, -real]
     right = jnp.concatenate([jnp.concatenate(right_real, 1), jnp.concatenate(right_imag, 1)], 0)
-    gram_ref[...] = lax.dot_general(
+    gram = lax.dot_general(
         jnp.concatenate(left, 1), right, (((1,), (1,)), ((), ())), precision=HIGH, preferred_element_type=F32
     )
+    row, lane = (lax.broadcasted_iota(jnp.int32, (NB, LANES), d) for d in range(2))
+    mixed = jnp.where(lane >= row, gram, pltpu.roll(gram, NB, 1))
+    half = NB // 2
+    packed = jnp.where(lane[:half] < NB, mixed[:half], pltpu.roll(mixed[half:], NB, 1))
+    energy = jnp.sum(q_ref[pl.ds(rows - 1, NB, stride=rows), :], axis=0, keepdims=True)
+    energy = jnp.where(row[:8] == 0, energy, 0.0)
+    for k in range(copies):
+        out_ref[k, :half, :] = packed
+        out_ref[k, half:, :] = energy
+
+
+def unpacked(parts_ref):
+    total = parts_ref[0]
+    for k in range(1, parts_ref.shape[0]):
+        total = total + parts_ref[k]
+    half = NB // 2
+    packed = total[:half]
+    row, lane = (lax.broadcasted_iota(jnp.int32, (NB, LANES), d) for d in range(2))
+    mixed = jnp.concatenate([packed, pltpu.roll(packed, NB, 1)], 0)
+    turned = jnp.transpose(jnp.concatenate([mixed, jnp.zeros_like(mixed)], 0))[:NB]
+    real = jnp.where(lane >= row, mixed, turned)
+    imag = jnp.where(lane < row, mixed, jnp.where(lane > row, -turned, 0.0))
+    return jnp.where(lane < NB, real, pltpu.roll(imag, NB, 1)), jnp.sum(total[half : half + 1], axis=1, keepdims=True)
 
 
 def rotate(state, offset, ranks):
@@ -122,9 +155,10 @@
     return new_top, new_bottom, new_dt, new_db
 
 
-def modes_kernel(gram_ref, q_ref, lam_ref, modes_ref, rows_ref):
+def modes_kernel(parts_ref, q_ref, modes_ref, spectrum_ref, gram_ref, rows_ref):
     lane = lax.broadcasted_iota(jnp.int32, (8, LANES), 1)
     sub = lax.broadcasted_iota(jnp.int32, (8, LANES), 0)
+    gram_ref[...], energy = unpacked(parts_ref)
     for v in range(GROUPS):
         for s in range(8):
             p = GROUPS * s + v
@@ -153,27 +187,32 @@
 
     flat = lax.fori_loop(0, SWEEPS * (NB - 1) // UNROLL, some_rounds, flat)
     top, bottom, diag_t, diag_b = jax.tree.unflatten(tree, flat)
+    eigen = jnp.zeros((8, LANES), F32)
+    left = lane < NB
     for v in range(GROUPS):
         for rows, diag, low in ((top[v], diag_t[v], True), (bottom[v], diag_b[v], False)):
             x, ix = rows[2], rows[3]
-            left = lane < NB
             sum_real = jnp.sum(jnp.where(left, x, 0.0), axis=1, keepdims=True)
             sum_imag = -jnp.sum(jnp.where(left, 0.0, x), axis=1, keepdims=True)
             magnitude = jnp.sqrt(sum_real * sum_real + sum_imag * sum_imag)
             scaling = 1.0 / (jnp.maximum(magnitude, 1.0) * jnp.sqrt(NB * (diag + 1e-06)))
             phase_r, phase_i = sum_real * scaling, -sum_imag * scaling
             coef = jnp.where(left, 1.0, -1.0) * (x * phase_r - ix * phase_i)
+            index = GROUPS * sub + v if low else 63 - GROUPS * sub - v
+            eigen = eigen + jnp.where(lane == index, diag, 0.0)
             for s in range(8):
                 p = GROUPS * s + v
                 row = p if low else 63 - p
                 rows_ref[row : row + 1, :] = coef[s : s + 1, :]
-                lam_ref[row : row + 1, :] = diag[s : s + 1, :]
-    nparts = q_ref.shape[0] // NB
+    spectrum = jnp.sum(eigen, axis=0, keepdims=True) * (NB * NB) / energy
+    spectrum_ref[...] = spectrum[:, :NB]
+    rows = q_ref.shape[0] // NB
+    nparts = rows - 1
     coefs = rows_ref[...]
     lhs = jnp.concatenate([coefs[:, :NB], coefs[:, NB:]], 0)
     for v in range(nparts // 2):
-        real = q_ref[pl.ds(2 * v, NB, stride=nparts), :]
-        imag = q_ref[pl.ds(2 * v + 1, NB, stride=nparts), :]
+        real = q_ref[pl.ds(2 * v, NB, stride=rows), :]
+        imag = q_ref[pl.ds(2 * v + 1, NB, stride=rows), :]
         out = jnp.dot(lhs, jnp.concatenate([real, imag], 1), precision=HIGH, preferred_element_type=F32)
         modes_ref[pl.ds(2 * v, NB, stride=nparts), :] = out[:NB, :LANES] - out[NB:, LANES:]
         modes_ref[pl.ds(2 * v + 1, NB, stride=nparts), :] = out[:NB, LANES:] + out[NB:, :LANES]
@@ -183,67 +222,60 @@
     return pl.BlockSpec(memory_space=space)
 
 
-def summed(part, axis):
-    size = lax.axis_size(axis)
-    step = 1
-    while step < size:
-        part = part + lax.ppermute(part, axis, [(i, i ^ step) for i in range(size)])
-        step *= 2
-    return part
+def half_spectra(tail, place, offsets, freqs, own):
+    nvars, nfft, npts = own.shape
+    return pl.pallas_call(
+        functools.partial(half_spectra_kernel, tail, nvars),
+        out_shape=jax.ShapeDtypeStruct((NB * 2 * nvars, npts), F32),
+        in_specs=[spec(pltpu.SMEM), spec(pltpu.SMEM), spec(pltpu.VMEM), spec(pltpu.HBM)],
+        scratch_shapes=[pltpu.VMEM((nvars, nfft, npts), F32), pltpu.SemaphoreType.DMA((nvars,))],
+        compiler_params=PARAMS,
+        cost_estimate=pl.CostEstimate(flops=12 * NB * 2 * nfft * nvars * npts, bytes_accessed=4 * own.size, transcendentals=0),
+        name="tail" if tail else "head",
+    )(place, offsets, freqs, own)
 
 
 def body(snapshots, weights, offsets, freqs):
     nfft, nvars, npts = snapshots.shape
     nfreq = freqs.shape[0]
     nblocks = lax.axis_size("blk")
-    total_pts = npts * lax.axis_size("pts")
-    block = lax.axis_index("blk").astype(jnp.int32).reshape(1)
+    nparts = lax.axis_size("pts")
+    rows = 2 * nvars + 1
+    place = lax.axis_index("blk").astype(jnp.int32).reshape(1)
     own = jnp.transpose(snapshots, (1, 0, 2))
-    route = [(i + 1, i) for i in range(nblocks - 1)]
-    following = lax.ppermute(own, "blk", route)
-    table = pl.pallas_call(
-        table_kernel,
-        out_shape=jax.ShapeDtypeStruct((2 * nfreq, nfft), F32),
-        in_specs=[spec(pltpu.SMEM), spec(pltpu.SMEM), spec(pltpu.VMEM)],
-        compiler_params=PARAMS,
-        name="table",
-    )(block, offsets, freqs.reshape(nfreq, 1))
-    scale = 1.0 / (nblocks * nvars * total_pts)
-    spectra, energy = pl.pallas_call(
-        functools.partial(spectra_kernel, scale),
-        out_shape=[
-            jax.ShapeDtypeStruct((nfreq * 2 * nvars, npts), F32),
-            jax.ShapeDtypeStruct((8, npts), F32),
-        ],
-        in_specs=[spec(pltpu.SMEM), spec(pltpu.SMEM)] + [spec(pltpu.VMEM)] * 4,
-        compiler_params=PARAMS,
-        name="spectra",
-    )(block, offsets, table, own, following, weights)
-    energies = lax.all_gather(energy, ("blk", "pts"), axis=0, tiled=True)
+    freqs = freqs.reshape(1, nfreq)
+    tail = half_spectra(True, place, offsets, freqs, own)
+    tail = lax.ppermute(tail, "blk", [(i + 1, i) for i in range(nblocks - 1)])
+    head = half_spectra(False, place, offsets, freqs, own)
+    scale = 1.0 / (nblocks * nvars * npts * nparts)
+    spectra = pl.pallas_call(
+        functools.partial(join_kernel, scale),
+        out_shape=jax.ShapeDtypeStruct((nfreq * rows, npts), F32),
+        compiler_params=PARAMS,
+        name="join",
+    )(head, tail, weights)
     grouped = lax.all_to_all(
-        spectra.reshape(nfreq, 1, nvars, 2, npts), "blk", split_axis=0, concat_axis=1, tiled=True
-    ).reshape(nblocks * 2 * nvars, npts)
+        spectra.reshape(nfreq, 1, rows, 1, npts), "blk", split_axis=0, concat_axis=1, tiled=True
+    ).reshape(nblocks * rows, npts)
     gram = pl.pallas_call(
-        functools.partial(gram_kernel, scale),
-        out_shape=jax.ShapeDtypeStruct((nblocks, 2 * nblocks), F32),
+        functools.partial(gram_kernel, scale, nparts),
+        out_shape=jax.ShapeDtypeStruct((nparts, nblocks // 2 + 8, LANES), F32),
         compiler_params=PARAMS,
         name="gram",
     )(grouped, weights)
-    gram = summed(gram, "pts")
-    lam, modes = pl.pallas_call(
+    parts = lax.all_to_all(gram, "pts", split_axis=0, concat_axis=0, tiled=True)
+    modes, spectrum = pl.pallas_call(
         modes_kernel,
         out_shape=[
-            jax.ShapeDtypeStruct((nblocks, LANES), F32),
             jax.ShapeDtypeStruct((nblocks * 2 * nvars, npts), F32),
+            jax.ShapeDtypeStruct((1, nblocks), F32),
         ],
-        scratch_shapes=[pltpu.VMEM((nblocks, LANES), F32)],
+        scratch_shapes=[pltpu.VMEM((nblocks, LANES), F32)] * 2,
         compiler_params=PARAMS,
         name="modes",
-    )(gram, grouped)
-    eigen = lam[:, 0].reshape(1, nblocks)
-    total = jnp.sum(energies)
+    )(parts, grouped)
     modes = modes.reshape(1, nblocks, nvars, 2, npts).transpose(0, 1, 3, 2, 4)
-    return modes, nfreq * nblocks * eigen / total
+    return modes, spectrum
 
 
 def solution(mesh):

time: 158 us -> 78.7 us (0.50)
  waiting for transfers between devices: 61.5 us -> 0.01 us
  starting transfers between devices: 27 us -> 8.79 us
  blocking collectives: 26 us -> 42.2 us
  between operations: 14.1 us -> 0.71 us
  other arithmetic: 4.08 us -> 0 us
  Pallas kernels: 20.8 us -> 24.7 us
  local copies, waits for them, and re-layouts: 3.83 us -> 1.75 us
    all_gather x1 -> x0, waiting for transfers between devices: 55.2 us -> none  [body(): energies = lax.all_gather(energy, ('blk', 'pts'), axis=0, tiled=True)]
    ppermute x4 -> x1, starting transfers between devices: 26.9 us -> 8.79 us  [body(): tail = lax.ppermute(tail, 'blk', [(i + 1, i) for i in range(nblocks - 1)])]
    all_to_all x1 -> x2, blocking collectives: 26 us -> 42.2 us  [the longest x1 23.7 us: body(): lax.all_to_all(spectra.reshape(nfreq, 1, rows, 1, npts), 'blk', split_axi...]
    ppermute x4 -> x1, waiting for transfers between devices: 6.29 us -> 0.01 us  [body(): tail = lax.ppermute(tail, 'blk', [(i + 1, i) for i in range(nblocks - 1)])]
    pallas_call x4 -> x5, Pallas kernels: 20.8 us -> 24.7 us  [the longest x1 17.5 us: body(): pl.pallas_call(modes_kernel, out_shape=[jax.ShapeDtypeStruct((nblocks * 2...]
    reduce_sum x1 -> x0, other arithmetic: 2.8 us -> none  [body(): total = jnp.sum(energies)]
  transfers between devices with their start and end apart: 5 -> 1, of which waited for: 5 -> 0; matrix products, arithmetic and copies ran while one was open for 0% -> 0% of each run, Pallas kernels for 12% -> 4%
where the time goes in v2:
time: 78.7 us; the launch traced here: 78.1 us
  blocking collectives  42.2 us (54%)
  Pallas kernels  24.7 us (31%)
  starting transfers between devices  8.79 us (11%)
  local copies, waits for them, and re-layouts  1.75 us (2%)
    all_to_all x1, blocking collectives, body(): lax.all_to_all(spectra.reshape(nfreq, 1, rows, 1, npts), 'blk', split_axi...  23.7 us
    all_to_all x1, blocking collectives, body(): parts = lax.all_to_all(gram, 'pts', split_axis=0, concat_axis=0, tiled=True)  18.5 us
    pallas_call x1, Pallas kernels, body(): pl.pallas_call(modes_kernel, out_shape=[jax.ShapeDtypeStruct((nblocks * 2...  17.5 us
    ppermute x1, starting transfers between devices, body(): tail = lax.ppermute(tail, 'blk', [(i + 1, i) for i in range(nblocks - 1)])  8.79 us
    pallas_call x2, Pallas kernels, half_spectra(): pl.pallas_call(functools.partial(half_spectra_kernel, tail, nvars), out_s...  6.23 us
    unnamed x8, local copies, waits for them, and re-layouts  1.75 us
  transfers between devices with their start and end apart: 1, of which 0 were waited for; matrix products, arithmetic and copies ran while one was open for 0% of the time, Pallas kernels for 4%

profile of v2, /device:TPU:1, one launch (start us, length us, event | category | flops | bytes accessed | tf_op | source)
XLA Modules:
  0.0 78.1 jit_solution(13756758691341832385)
XLA Ops:
  0.6 0.0 copy-start.2
  0.6 0.0 copy-start.3
  0.7 0.6 copy-done.2
  1.3 0.0 copy-done.3
  1.3 0.0 copy-start
  1.3 1.1 %copy-done = f32[256,5,128]{2,0,1:T(8,128)S(1)} copy-done((f32[256,5,128]{2,0,1:T(8,128)S(1)}, f32[256,5,128]{2,0,1:T(8,128)}, u32[]{:S(2)}) %copy-start) | copy-done | bytes 655384
  2.4 3.1 %tail.1 = f32[640,128]{1,0:T(8,128)S(1)} custom-call(s32[1]{0:T(128)} %bitcast.place_ref, s32[64]{0:T(128)S(1)} %copy-done.2, s32[1,64]{1,0:T(1,128)S(1)} %bitcast.13, f32[5,256,128]{2,1,0:T(8,128)S(1)} %bitcast.10), custom_call_target="tpu_custom_call" | custom-call | flops 251658240 | bytes 655360 | tf_op jit(solution)/shard_map/tail/pallas_call | solution.py:227
  5.5 0.0 copy-start.1
  5.5 8.8 %collective-permute-start = (f32[640,128]{1,0:T(8,128)S(1)}, f32[640,128]{1,0:T(8,128)S(1)}, u32[]{:S(2)}, u32[]{:S(2)}) collective-permute-start(f32[640,128]{1,0:T(8,128)S(1)} %tail.1), channel_id=1, source_target_pairs={{8,0},{16,8},{24,16},{32,24},{40,32},{48,40},{56,48},{64,56},{72,6... | collective-permute-start | bytes 983048 | tf_op jit(solution)/shard_map/ppermute | solution.py:248
  14.3 3.1 %head.1.head_ref = f32[640,128]{1,0:T(8,128)S(1)} custom-call(s32[1]{0:T(128)} %bitcast.place_ref, s32[64]{0:T(128)S(1)} %copy-done.2, s32[1,64]{1,0:T(1,128)S(1)} %bitcast.14, f32[5,256,128]{2,1,0:T(8,128)S(1)} %bitcast.11), custom_call_target="tpu_custom_call" | custom-call | flops 251658240 | bytes 655360 | tf_op jit(solution)/shard_map/head/pallas_call | solution.py:227
  17.5 0.0 collective-permute-done.tail_ref
  17.5 0.0 copy-done.1
  17.5 0.1 join.1
  17.5 23.7 %all_to_all.14 = f32[64,1,11,1,128]{4,3,2,1,0:T(1,128)S(1)} all-to-all(f32[64,1,11,1,128]{4,3,2,1,0:T(1,128)S(1)} %bitcast.12), channel_id=1, replica_groups=mesh['blk'=64,'pts'=8] {'blk'}, dimensions={0} | all-to-all | bytes 720896 | tf_op jit(solution)/shard_map/all_to_all | solution.py:257
  41.2 0.9 %gram.1 = f32[8,40,128]{2,1,0:T(8,128)S(1)} custom-call(f32[704,128]{1,0:T(8,128)S(1)} %bitcast.8, f32[5,128]{1,0:T(8,128)S(1)} %copy-done.1), custom_call_target="tpu_custom_call" | custom-call | tf_op jit(solution)/shard_map/gram/pallas_call | solution.py:260
  42.1 18.5 %all_to_all.15.parts_ref = f32[8,40,128]{2,1,0:T(8,128)S(1)} all-to-all(f32[8,40,128]{2,1,0:T(8,128)S(1)} %gram.1), channel_id=1, replica_groups=mesh['blk'=64,'pts'=8] {'pts'}, dimensions={0} | all-to-all | bytes 327680 | tf_op jit(solution)/shard_map/all_to_all | solution.py:266
  60.7 17.5 %modes.1 = (f32[640,128]{1,0:T(8,128)}, f32[1,64]{1,0:T(1,128)}) custom-call(f32[8,40,128]{2,1,0:T(8,128)S(1)} %all_to_all.15.parts_ref, f32[704,128]{1,0:T(8,128)S(1)} %bitcast.9), custom_call_target="tpu_custom_call" | custom-call | tf_op jit(solution)/shard_map/modes/pallas_call | solution.py:267
Async XLA Ops:
  0.6 0.7 copy-start.2
  0.6 0.7 copy-start.3
  1.3 1.1 %copy-start = (f32[256,5,128]{2,0,1:T(8,128)S(1)}, f32[256,5,128]{2,0,1:T(8,128)}, u32[]{:S(2)}) copy-start(f32[256,5,128]{2,0,1:T(8,128)} %param.4) | copy-start | bytes 1966084
  5.5 11.9 %copy-start.1 = (f32[5,128]{1,0:T(8,128)S(1)}, f32[5,128]{1,0:T(8,128)}, u32[]{:S(2)}) copy-start(f32[5,128]{1,0:T(8,128)} %weights_ref.3) | copy-start | bytes 7684
  5.5 11.9 %collective-permute-start = (f32[640,128]{1,0:T(8,128)S(1)}, f32[640,128]{1,0:T(8,128)S(1)}, u32[]{:S(2)}, u32[]{:S(2)}) collective-permute-start(f32[640,128]{1,0:T(8,128)S(1)} %tail.1), channel_id=1, source_target_pairs={{8,0},{16,8},{24,16},{32,24},{40,32},{48,40},{56,48},{64,56},{72,6... | collective-permute-start | bytes 983048 | tf_op jit(solution)/shard_map/ppermute | solution.py:248

commit v3 on v2

--- a/solution.py
+++ b/solution.py
@@ -20,12 +20,20 @@
 PARAMS = pltpu.CompilerParams(vmem_limit_bytes=16 << 20)
 
 
-def half_spectra_kernel(tail, nvars, place_ref, offsets_ref, freqs_ref, own_ref, out_ref, data_ref, sem):
+def half_spectra_kernel(tail, nvars, offsets_hbm, freqs_hbm, own_ref, out_ref, offsets_ref, freqs_ref, data_ref, sem):
+    small = [
+        pltpu.make_async_copy(offsets_hbm, offsets_ref, sem.at[nvars]),
+        pltpu.make_async_copy(freqs_hbm, freqs_ref, sem.at[nvars + 1]),
+    ]
     copies = [pltpu.make_async_copy(own_ref.at[v], data_ref.at[v], sem.at[v]) for v in range(nvars)]
-    for copy in copies:
+    for copy in small + copies:
         copy.start()
-    block = place_ref[0]
-    offset = offsets_ref[jnp.maximum(block - 1, 0) if tail else block]
+    block = lax.axis_index("blk")
+    if tail:
+        block = jnp.where(block == 0, NB, block) - 1
+    for copy in small:
+        copy.wait()
+    offset = offsets_ref[0, block]
     snapshot = lax.broadcasted_iota(jnp.int32, (1, NFFT), 1)
     lag = jnp.bitwise_and(snapshot - offset, NFFT - 1)
     valid = snapshot < offset if tail else snapshot >= offset
@@ -36,11 +44,14 @@
     freqs = jnp.sum(jnp.where(same, freqs_ref[...].astype(F32), 0.0), axis=1, keepdims=True).astype(jnp.int32)
     angle = unit * jnp.bitwise_and(freqs * lag, NFFT - 1).astype(F32)
     table = jnp.concatenate([hann * jnp.cos(angle), -hann * jnp.sin(angle)], 0)
+    for copy in copies:
+        copy.wait()
+    data = jnp.concatenate([data_ref[v] for v in range(nvars)], 1)
+    result = jnp.dot(table, data, precision=HIGH, preferred_element_type=F32)
     for v in range(nvars):
-        copies[v].wait()
-        result = jnp.dot(table, data_ref[v], precision=HIGH, preferred_element_type=F32)
         for part in range(2):
-            out_ref[pl.ds(2 * v + part, NB, stride=2 * nvars), :] = result[part * NB : (part + 1) * NB]
+            piece = result[part * NB : (part + 1) * NB, v * LANES : (v + 1) * LANES]
+            out_ref[pl.ds(2 * v + part, NB, stride=2 * nvars), :] = piece
 
 
 def join_kernel(scale, head_ref, tail_ref, weights_ref, out_ref):
@@ -95,64 +106,72 @@
     return jnp.where(lane < NB, real, pltpu.roll(imag, NB, 1)), jnp.sum(total[half : half + 1], axis=1, keepdims=True)
 
 
-def rotate(state, offset, ranks):
-    top, bottom, diag_t, diag_b = state
-    new_top, new_bottom, new_dt, new_db = [], [], [], []
-    for v in range(GROUPS):
-        zt, izt, xt, ixt = top[v]
-        zb, izb, xb, ixb = bottom[v]
-        real = jnp.sum(zt * xb, axis=1, keepdims=True)
-        imag = jnp.sum(zt * ixb, axis=1, keepdims=True)
+def shift_top(tops, bottoms, row):
+    return [tops[1], tops[2], tops[3], jnp.where(row == 7, bottoms, pltpu.roll(tops[0], 7, 0))]
+
+
+def shift_bottom(tops, bottoms, row):
+    first = jnp.where(row == 0, bottoms[0], pltpu.roll(bottoms[3], 1, 0))
+    second = bottoms[0] if tops is None else jnp.where(row == 0, tops, bottoms[0])
+    return [first, second, bottoms[1], bottoms[2]]
+
+
+def one_round(state, offset, ranks, row):
+    top, bottom, diag_t, diag_b, beta = state
+
+    def col(rows, i):
+        return [r[i] for r in rows]
+
+    total = lambda x: jnp.sum(x, axis=1, keepdims=True)
+    tz, bz = col(top, 0), col(bottom, 0)
+    uz, wz = shift_top(tz, bz[3], row), shift_top(bz, tz[3], row)
+    ux, uix, wx, wix = [], [], [], []
+    for i, (u, w) in ((2, (ux, wx)), (3, (uix, wix))):
+        t, b = col(top, i), col(bottom, i)
+        u += shift_bottom(t[0], b, row)
+        w += shift_bottom(b[0], t, row)
+    inner = []
+    for v in range(GROUPS):
+        inner.append([(total(z * x), total(z * ix)) for z in (uz[v], wz[v]) for x, ix in ((ux[v], uix[v]), (wx[v], wix[v]))])
+    cos, off, img, new_dt, new_db = [], [], [], [], []
+    wide = lambda x: jnp.broadcast_to(x, (8, LANES))
+    new_top, new_bottom = [], []
+    for v in range(GROUPS):
+        real, imag = beta[v]
         at, ab = diag_t[v], diag_b[v]
         sign = jnp.where(ranks[v] > offset, 1.0, -1.0)
-        delta = sign * (ab - at)
+        gap = ab - at
+        delta = sign * gap
         four = 4.0 * (real * real + imag * imag)
         square = delta * delta + four
         radius = square * lax.rsqrt(jnp.maximum(square, 1e-37))
-        upper = radius + delta + DAMPING * (ab + at)
+        upper = radius + (delta + DAMPING * (ab + at))
         inverse = lax.rsqrt(upper * upper + four)
-        cosine = upper * inverse
+        c = upper * inverse
         twice = (sign + sign) * inverse
-        off_r, off_i = twice * real, twice * imag
-        cc = cosine * cosine
-        oo = off_r * off_r + off_i * off_i
-        cross = (cosine + cosine) * (off_r * real + off_i * imag)
-        new_dt.append(cc * at + oo * ab - cross)
-        new_db.append(cc * ab + oo * at + cross)
-        new_top.append(
-            (
-                cosine * zt - off_r * zb - off_i * izb,
-                cosine * izt - off_r * izb + off_i * zb,
-                cosine * xt - off_r * xb - off_i * ixb,
-                cosine * ixt - off_r * ixb + off_i * xb,
-            )
-        )
-        new_bottom.append(
-            (
-                cosine * zb + off_r * zt - off_i * izt,
-                cosine * izb + off_r * izt + off_i * zt,
-                cosine * xb + off_r * xt - off_i * ixt,
-                cosine * ixb + off_r * ixt + off_i * xt,
-            )
-        )
-    return new_top, new_bottom, new_dt, new_db
-
-
-def advance(state):
-    top, bottom, diag_t, diag_b = state
-    row = lax.broadcasted_iota(jnp.int32, (8, LANES), 0)
-
-    def ring(tops, bottoms):
-        last = jnp.where(row == 7, bottoms[3], pltpu.roll(tops[0], 7, 0))
-        first = jnp.where(row == 0, bottoms[0], pltpu.roll(bottoms[3], 1, 0))
-        second = jnp.where(row == 0, tops[0], bottoms[0])
-        return [tops[1], tops[2], tops[3], last], [first, second, bottoms[1], bottoms[2]]
-
-    parts = [ring([t[i] for t in top], [b[i] for b in bottom]) for i in range(4)]
-    new_top = [tuple(parts[i][0][v] for i in range(4)) for v in range(GROUPS)]
-    new_bottom = [tuple(parts[i][1][v] for i in range(4)) for v in range(GROUPS)]
-    new_dt, new_db = ring(diag_t, diag_b)
-    return new_top, new_bottom, new_dt, new_db
+        r, i = twice * real, twice * imag
+        moved = (four * inverse) * (inverse * gap - sign * c)
+        new_dt.append(at + moved)
+        new_db.append(ab - moved)
+        cos.append(c); off.append(r); img.append(i)
+        (zt, izt, xt, ixt), (zb, izb, xb, ixb) = top[v], bottom[v]
+        new_top.append((c * zt - r * zb - i * izb, c * izt - r * izb + i * zb, c * xt - r * xb - i * ixb, c * ixt - r * ixb + i * xb))
+        new_bottom.append((c * zb + r * zt - i * izt, c * izb + r * izt + i * zt, c * xb + r * xt - i * ixt, c * ixb + r * ixt + i * xt))
+    c1, r1, i1 = shift_top(cos, cos[3], row), shift_top(off, -off[3], row), shift_top(img, img[3], row)
+    c2, r2, i2 = shift_bottom(None, cos, row), shift_bottom(-off[0], off, row), shift_bottom(None, img, row)
+    new_beta = []
+    for v in range(GROUPS):
+        uu, uw, wu, ww = inner[v]
+        ca, ra, ia, cb, rb, ib = c1[v], r1[v], i1[v], c2[v], r2[v], i2[v]
+        ur = cb * uu[0] + rb * uw[0] - ib * uw[1]
+        ui = cb * uu[1] + rb * uw[1] + ib * uw[0]
+        wr = cb * wu[0] + rb * ww[0] - ib * ww[1]
+        wi = cb * wu[1] + rb * ww[1] + ib * ww[0]
+        new_beta.append((wide(ca * ur - ra * wr + ia * wi), wide(ca * ui - ra * wi - ia * wr)))
+    tops = [shift_top(col(new_top, i), new_bottom[3][i], row) for i in range(4)]
+    bottoms = [shift_bottom(new_top[0][i], col(new_bottom, i), row) for i in range(4)]
+    return (list(zip(*tops)), list(zip(*bottoms)), shift_top(new_dt, new_db[3], row),
+            shift_bottom(new_dt[0], new_db, row), new_beta)
 
 
 def modes_kernel(parts_ref, q_ref, modes_ref, spectrum_ref, gram_ref, rows_ref):
@@ -175,18 +194,22 @@
             rows.append((z, flip * pltpu.roll(z, NB, 1), x, ix))
             diag.append(jnp.broadcast_to(jnp.sum(z * x, axis=1, keepdims=True), (8, LANES)))
         ranks.append(jnp.where(p == 0, 1000, p))
-    flat, tree = jax.tree.flatten((top, bottom, diag_t, diag_b))
+    def inner(z, x):
+        return jnp.broadcast_to(jnp.sum(z * x, axis=1, keepdims=True), (8, LANES))
+
+    beta = [(inner(t[0], b[2]), inner(t[0], b[3])) for t, b in zip(top, bottom)]
+    flat, tree = jax.tree.flatten((top, bottom, diag_t, diag_b, beta))
 
     def some_rounds(step, flat):
         state = jax.tree.unflatten(tree, flat)
         base = lax.rem(step * UNROLL, NB - 1)
         for i in range(UNROLL):
             offset = 31 - jnp.abs(base + i - 31)
-            state = advance(rotate(state, offset, ranks))
+            state = one_round(state, offset, ranks, sub)
         return jax.tree.flatten(state)[0]
 
     flat = lax.fori_loop(0, SWEEPS * (NB - 1) // UNROLL, some_rounds, flat)
-    top, bottom, diag_t, diag_b = jax.tree.unflatten(tree, flat)
+    top, bottom, diag_t, diag_b, _ = jax.tree.unflatten(tree, flat)
     eigen = jnp.zeros((8, LANES), F32)
     left = lane < NB
     for v in range(GROUPS):
@@ -222,17 +245,22 @@
     return pl.BlockSpec(memory_space=space)
 
 
-def half_spectra(tail, place, offsets, freqs, own):
+def half_spectra(tail, offsets, freqs, own):
     nvars, nfft, npts = own.shape
     return pl.pallas_call(
         functools.partial(half_spectra_kernel, tail, nvars),
         out_shape=jax.ShapeDtypeStruct((NB * 2 * nvars, npts), F32),
-        in_specs=[spec(pltpu.SMEM), spec(pltpu.SMEM), spec(pltpu.VMEM), spec(pltpu.HBM)],
-        scratch_shapes=[pltpu.VMEM((nvars, nfft, npts), F32), pltpu.SemaphoreType.DMA((nvars,))],
-        compiler_params=PARAMS,
+        in_specs=[spec(pl.ANY)] * 3,
+        scratch_shapes=[
+            pltpu.SMEM(offsets.shape, jnp.int32),
+            pltpu.VMEM(freqs.shape, jnp.int32),
+            pltpu.VMEM((nvars, nfft, npts), F32),
+            pltpu.SemaphoreType.DMA((nvars + 2,)),
+        ],
+        compiler_params=pltpu.CompilerParams(vmem_limit_bytes=(60 if tail else 16) << 20),
         cost_estimate=pl.CostEstimate(flops=12 * NB * 2 * nfft * nvars * npts, bytes_accessed=4 * own.size, transcendentals=0),
         name="tail" if tail else "head",
-    )(place, offsets, freqs, own)
+    )(offsets, freqs, own)
 
 
 def body(snapshots, weights, offsets, freqs):
@@ -241,12 +269,12 @@
     nblocks = lax.axis_size("blk")
     nparts = lax.axis_size("pts")
     rows = 2 * nvars + 1
-    place = lax.axis_index("blk").astype(jnp.int32).reshape(1)
     own = jnp.transpose(snapshots, (1, 0, 2))
     freqs = freqs.reshape(1, nfreq)
-    tail = half_spectra(True, place, offsets, freqs, own)
-    tail = lax.ppermute(tail, "blk", [(i + 1, i) for i in range(nblocks - 1)])
-    head = half_spectra(False, place, offsets, freqs, own)
+    offsets = offsets.reshape(1, nblocks)
+    tail = half_spectra(True, offsets, freqs, own)
+    tail = lax.ppermute(tail, "blk", [(i, (i - 1) % nblocks) for i in range(nblocks)])
+    head = half_spectra(False, offsets, freqs, own)
     scale = 1.0 / (nblocks * nvars * npts * nparts)
     spectra = pl.pallas_call(
         functools.partial(join_kernel, scale),

time: 78.7 us -> 72.7 us (0.924)
  Pallas kernels: 24.7 us -> 18.9 us
  local copies, waits for them, and re-layouts: 1.75 us -> 0.02 us
  blocking collectives: 42.2 us -> 43.7 us
    pallas_call x1, Pallas kernels: 17.5 us -> 13.6 us  [body(): pl.pallas_call(modes_kernel, out_shape=[jax.ShapeDtypeStruct((nblocks * 2...]
    pallas_call x2, Pallas kernels: 6.23 us -> 4.35 us  [half_spectra(): pl.pallas_call(functools.partial(half_spectra_kernel, tail, nvars), out_s...]
    unnamed x8, local copies, waits for them, and re-layouts: 1.75 us -> 0.02 us
    all_to_all x1, blocking collectives: 23.7 us -> 25.2 us  [body(): lax.all_to_all(spectra.reshape(nfreq, 1, rows, 1, npts), 'blk', split_axi...]
  transfers between devices with their start and end apart: 1 -> 1, of which waited for: 0 -> 0; matrix products, arithmetic and copies ran while one was open for 0% -> 0% of each run, Pallas kernels for 4% -> 3%
where the time goes in v3:
time: 72.7 us; the launch traced here: 72.2 us
  blocking collectives  43.7 us (60%)
  Pallas kernels  18.9 us (26%)
  starting transfers between devices  8.79 us (12%)
  between operations  0.73 us (1%)
    all_to_all x1, blocking collectives, body(): lax.all_to_all(spectra.reshape(nfreq, 1, rows, 1, npts), 'blk', split_axi...  25.2 us
    all_to_all x1, blocking collectives, body(): parts = lax.all_to_all(gram, 'pts', split_axis=0, concat_axis=0, tiled=True)  18.5 us
    pallas_call x1, Pallas kernels, body(): pl.pallas_call(modes_kernel, out_shape=[jax.ShapeDtypeStruct((nblocks * 2...  13.6 us
    ppermute x1, starting transfers between devices, body(): lax.ppermute(tail, 'blk', [(i, (i - 1) % nblocks) for i in range(nblocks)])  8.79 us
    pallas_call x2, Pallas kernels, half_spectra(): pl.pallas_call(functools.partial(half_spectra_kernel, tail, nvars), out_s...  4.35 us
  transfers between devices with their start and end apart: 1, of which 0 were waited for; matrix products, arithmetic and copies ran while one was open for 0% of the time, Pallas kernels for 3%

profile of v3, /device:TPU:1, one launch (start us, length us, event | category | flops | bytes accessed | tf_op | source)
XLA Modules:
  0.0 72.2 jit_solution(10952417909090605772)
XLA Ops:
  0.6 0.0 copy-start
  0.6 0.0 copy-start.2
  0.6 0.0 copy-start.3
  0.7 2.5 %tail.1 = f32[640,128]{1,0:T(8,128)} custom-call(s32[1,64]{1,0:T(1,128)} %bitcast.13, s32[1,64]{1,0:T(1,128)} %bitcast.15, f32[5,256,128]{2,1,0:T(8,128)} %bitcast.10), custom_call_target="tpu_custom_call" | custom-call | flops 251658240 | bytes 655360 | tf_op jit(solution)/shard_map/tail/pallas_call | solution.py:250
  3.2 0.0 copy-start.1
  3.2 8.8 %collective-permute-start = (f32[640,128]{1,0:T(8,128)}, f32[640,128]{1,0:T(8,128)S(1)}, u32[]{:S(2)}, u32[]{:S(2)}) collective-permute-start(f32[640,128]{1,0:T(8,128)} %tail.1), channel_id=1, source_target_pairs={{0,504},{8,0},{16,8},{24,16},{32,24},{40,32},{48,40},{56,48},{64,5... | collective-permute-start | bytes 983048 | tf_op jit(solution)/shard_map/ppermute | solution.py:276
  12.0 0.0 copy-done
  12.0 0.0 copy-done.2
  12.0 0.0 copy-done.3
  12.1 1.8 %head.1.head_ref = f32[640,128]{1,0:T(8,128)S(1)} custom-call(s32[1,64]{1,0:T(1,128)S(1)} %bitcast.14, s32[1,64]{1,0:T(1,128)S(1)} %bitcast.16, f32[5,256,128]{2,1,0:T(8,128)S(1)} %bitcast.11), custom_call_target="tpu_custom_call" | custom-call | flops 251658240 | bytes 655360 | tf_op jit(solution)/shard_map/head/pallas_call | solution.py:250
  13.9 0.0 collective-permute-done.tail_ref
  13.9 0.0 copy-done.1
  13.9 0.1 join.1
  14.0 25.2 %all_to_all.14 = f32[64,1,11,1,128]{4,3,2,1,0:T(1,128)S(1)} all-to-all(f32[64,1,11,1,128]{4,3,2,1,0:T(1,128)S(1)} %bitcast.12), channel_id=1, replica_groups=mesh['blk'=64,'pts'=8] {'blk'}, dimensions={0} | all-to-all | bytes 720896 | tf_op jit(solution)/shard_map/all_to_all | solution.py:285
  39.1 0.9 %gram.1 = f32[8,40,128]{2,1,0:T(8,128)S(1)} custom-call(f32[704,128]{1,0:T(8,128)S(1)} %bitcast.8, f32[5,128]{1,0:T(8,128)S(1)} %copy-done.1), custom_call_target="tpu_custom_call" | custom-call | tf_op jit(solution)/shard_map/gram/pallas_call | solution.py:288
  40.0 18.5 %all_to_all.15.parts_ref = f32[8,40,128]{2,1,0:T(8,128)S(1)} all-to-all(f32[8,40,128]{2,1,0:T(8,128)S(1)} %gram.1), channel_id=1, replica_groups=mesh['blk'=64,'pts'=8] {'pts'}, dimensions={0} | all-to-all | bytes 327680 | tf_op jit(solution)/shard_map/all_to_all | solution.py:294
  58.6 13.6 %modes.1 = (f32[640,128]{1,0:T(8,128)}, f32[1,64]{1,0:T(1,128)}) custom-call(f32[8,40,128]{2,1,0:T(8,128)S(1)} %all_to_all.15.parts_ref, f32[704,128]{1,0:T(8,128)S(1)} %bitcast.9), custom_call_target="tpu_custom_call" | custom-call | tf_op jit(solution)/shard_map/modes/pallas_call | solution.py:295
Async XLA Ops:
  0.6 11.4 %copy-start = (f32[256,5,128]{2,0,1:T(8,128)S(1)}, f32[256,5,128]{2,0,1:T(8,128)}, u32[]{:S(2)}) copy-start(f32[256,5,128]{2,0,1:T(8,128)} %param.4) | copy-start | bytes 1966084
  0.6 11.4 %copy-start.2 = (s32[64]{0:T(128)S(1)}, s32[64]{0:T(128)}, u32[]{:S(2)}) copy-start(s32[64]{0:T(128)} %param.6) | copy-start | bytes 772
  0.6 11.4 %copy-start.3 = (s32[64]{0:T(128)S(1)}, s32[64]{0:T(128)}, u32[]{:S(2)}) copy-start(s32[64]{0:T(128)} %param.7) | copy-start | bytes 772
  3.2 10.7 %copy-start.1 = (f32[5,128]{1,0:T(8,128)S(1)}, f32[5,128]{1,0:T(8,128)}, u32[]{:S(2)}) copy-start(f32[5,128]{1,0:T(8,128)} %weights_ref.3) | copy-start | bytes 7684
  3.2 10.6 %collective-permute-start = (f32[640,128]{1,0:T(8,128)}, f32[640,128]{1,0:T(8,128)S(1)}, u32[]{:S(2)}, u32[]{:S(2)}) collective-permute-start(f32[640,128]{1,0:T(8,128)} %tail.1), channel_id=1, source_target_pairs={{0,504},{8,0},{16,8},{24,16},{32,24},{40,32},{48,40},{56,48},{64,5... | collective-permute-start | bytes 983048 | tf_op jit(solution)/shard_map/ppermute | solution.py:276

commit v4 on v3

--- a/solution.py
+++ b/solution.py
@@ -16,7 +16,7 @@
 NB = 64
 LANES = 128
 GROUPS = 4
-UNROLL = 7
+UNROLL = 20
 PARAMS = pltpu.CompilerParams(vmem_limit_bytes=16 << 20)
 
 
@@ -66,21 +66,32 @@
     out_ref[pl.ds(rows - 1, NB, stride=rows), :] = jnp.broadcast_to(energy, (NB, LANES))
 
 
+def thirds(x):
+    high = x.astype(jnp.bfloat16)
+    rest = x - high.astype(F32)
+    middle = rest.astype(jnp.bfloat16)
+    return high, middle, (rest - middle.astype(F32)).astype(jnp.bfloat16)
+
+
 def gram_kernel(scale, copies, q_ref, weights_ref, out_ref):
     nvars = weights_ref.shape[0]
     rows = 2 * nvars + 1
-    left, right_real, right_imag = [], [], []
+    left, right_real, right_imag = ([], [], []), ([], [], []), ([], [], [])
     for v in range(nvars):
         real = q_ref[pl.ds(2 * v, NB, stride=rows), :]
         imag = q_ref[pl.ds(2 * v + 1, NB, stride=rows), :]
         weight = weights_ref[v : v + 1, :] * scale
-        left += [real * weight, imag * weight]
-        right_real += [real, imag]
-        right_imag += [imag, -real]
-    right = jnp.concatenate([jnp.concatenate(right_real, 1), jnp.concatenate(right_imag, 1)], 0)
-    gram = lax.dot_general(
-        jnp.concatenate(left, 1), right, (((1,), (1,)), ((), ())), precision=HIGH, preferred_element_type=F32
-    )
+        terms = zip(thirds(real * weight), thirds(imag * weight), thirds(real), thirds(imag))
+        for k, (weighted_real, weighted_imag, real, imag) in enumerate(terms):
+            left[k].extend((weighted_real, weighted_imag))
+            right_real[k].extend((real, imag))
+            right_imag[k].extend((imag, -real))
+    lhs = jnp.concatenate([jnp.concatenate(term, 1) for term in left], 0)
+    rhs = jnp.concatenate([jnp.concatenate(term, 1) for pair in zip(right_real, right_imag) for term in pair], 0)
+    product = lax.dot_general(lhs, rhs, (((1,), (1,)), ((), ())), preferred_element_type=F32)
+    gram = 0.0
+    for i, k in ((1, 1), (0, 2), (2, 0), (0, 1), (1, 0), (0, 0)):
+        gram = gram + product[i * NB : (i + 1) * NB, k * LANES : (k + 1) * LANES]
     row, lane = (lax.broadcasted_iota(jnp.int32, (NB, LANES), d) for d in range(2))
     mixed = jnp.where(lane >= row, gram, pltpu.roll(gram, NB, 1))
     half = NB // 2
@@ -140,19 +151,17 @@
         real, imag = beta[v]
         at, ab = diag_t[v], diag_b[v]
         sign = jnp.where(ranks[v] > offset, 1.0, -1.0)
-        gap = ab - at
-        delta = sign * gap
-        four = 4.0 * (real * real + imag * imag)
+        delta = sign * (ab - at)
+        four = real * real + imag * imag
         square = delta * delta + four
-        radius = square * lax.rsqrt(jnp.maximum(square, 1e-37))
-        upper = radius + (delta + DAMPING * (ab + at))
+        high = square * lax.rsqrt(jnp.maximum(square, 1e-37)) + DAMPING * (ab + at)
+        upper = high + delta
         inverse = lax.rsqrt(upper * upper + four)
-        c = upper * inverse
-        twice = (sign + sign) * inverse
-        r, i = twice * real, twice * imag
-        moved = (four * inverse) * (inverse * gap - sign * c)
-        new_dt.append(at + moved)
-        new_db.append(ab - moved)
+        signed = sign * inverse
+        c, r, i = upper * inverse, signed * real, signed * imag
+        moved = (four * inverse) * (signed * high)
+        new_dt.append(at - moved)
+        new_db.append(ab + moved)
         cos.append(c); off.append(r); img.append(i)
         (zt, izt, xt, ixt), (zb, izb, xb, ixb) = top[v], bottom[v]
         new_top.append((c * zt - r * zb - i * izb, c * izt - r * izb + i * zb, c * xt - r * xb - i * ixb, c * ixt - r * ixb + i * xb))
@@ -174,6 +183,11 @@
             shift_bottom(new_dt[0], new_db, row), new_beta)
 
 
+def split(x):
+    high = x.astype(jnp.bfloat16)
+    return high, (x - high.astype(F32)).astype(jnp.bfloat16)
+
+
 def modes_kernel(parts_ref, q_ref, modes_ref, spectrum_ref, gram_ref, rows_ref):
     lane = lax.broadcasted_iota(jnp.int32, (8, LANES), 1)
     sub = lax.broadcasted_iota(jnp.int32, (8, LANES), 0)
@@ -191,7 +205,7 @@
             z = rows_ref[base + 8 * v : base + 8 * v + 8, :]
             x = jnp.where(lane == index, 1.0, 0.0)
             ix = jnp.where(lane == index + NB, 1.0, 0.0)
-            rows.append((z, flip * pltpu.roll(z, NB, 1), x, ix))
+            rows.append((z + z, (flip + flip) * pltpu.roll(z, NB, 1), x, ix))
             diag.append(jnp.broadcast_to(jnp.sum(z * x, axis=1, keepdims=True), (8, LANES)))
         ranks.append(jnp.where(p == 0, 1000, p))
     def inner(z, x):
@@ -202,14 +216,17 @@
 
     def some_rounds(step, flat):
         state = jax.tree.unflatten(tree, flat)
-        base = lax.rem(step * UNROLL, NB - 1)
         for i in range(UNROLL):
-            offset = 31 - jnp.abs(base + i - 31)
+            offset = 31 - jnp.abs(lax.rem(step * UNROLL + i, NB - 1) - 31)
             state = one_round(state, offset, ranks, sub)
         return jax.tree.flatten(state)[0]
 
-    flat = lax.fori_loop(0, SWEEPS * (NB - 1) // UNROLL, some_rounds, flat)
-    top, bottom, diag_t, diag_b, _ = jax.tree.unflatten(tree, flat)
+    rounds = SWEEPS * (NB - 1)
+    flat = lax.fori_loop(0, rounds // UNROLL, some_rounds, flat)
+    state = jax.tree.unflatten(tree, flat)
+    for i in range(rounds // UNROLL * UNROLL, rounds):
+        state = one_round(state, 31 - abs(i % (NB - 1) - 31), ranks, sub)
+    top, bottom, diag_t, diag_b, _ = state
     eigen = jnp.zeros((8, LANES), F32)
     left = lane < NB
     for v in range(GROUPS):
@@ -232,11 +249,13 @@
     rows = q_ref.shape[0] // NB
     nparts = rows - 1
     coefs = rows_ref[...]
-    lhs = jnp.concatenate([coefs[:, :NB], coefs[:, NB:]], 0)
+    high, low = split(jnp.concatenate([coefs[:, :NB], coefs[:, NB:]], 0))
+    lhs = jnp.concatenate([high, high, low], 1)
     for v in range(nparts // 2):
         real = q_ref[pl.ds(2 * v, NB, stride=rows), :]
         imag = q_ref[pl.ds(2 * v + 1, NB, stride=rows), :]
-        out = jnp.dot(lhs, jnp.concatenate([real, imag], 1), precision=HIGH, preferred_element_type=F32)
+        high, low = split(jnp.concatenate([real, imag], 1))
+        out = jnp.dot(lhs, jnp.concatenate([high, low, high], 0), preferred_element_type=F32)
         modes_ref[pl.ds(2 * v, NB, stride=nparts), :] = out[:NB, :LANES] - out[NB:, LANES:]
         modes_ref[pl.ds(2 * v + 1, NB, stride=nparts), :] = out[:NB, LANES:] + out[NB:, :LANES]
 
@@ -273,7 +292,7 @@
     freqs = freqs.reshape(1, nfreq)
     offsets = offsets.reshape(1, nblocks)
     tail = half_spectra(True, offsets, freqs, own)
-    tail = lax.ppermute(tail, "blk", [(i, (i - 1) % nblocks) for i in range(nblocks)])
+    tail = lax.ppermute(tail, "blk", [(i + 1, i) for i in range(nblocks - 1)])
     head = half_spectra(False, offsets, freqs, own)
     scale = 1.0 / (nblocks * nvars * npts * nparts)
     spectra = pl.pallas_call(

time: 72.7 us -> 70.4 us (0.968)
  Pallas kernels: 18.9 us -> 16.6 us
    pallas_call x1, Pallas kernels: 13.6 us -> 11.5 us  [body(): pl.pallas_call(modes_kernel, out_shape=[jax.ShapeDtypeStruct((nblocks * 2...]
where the time goes in v4:
time: 70.4 us; the launch traced here: 69.8 us
  blocking collectives  43.7 us (62%)
  Pallas kernels  16.6 us (24%)
  starting transfers between devices  8.79 us (12%)
  between operations  0.73 us (1%)
    all_to_all x1, blocking collectives, body(): lax.all_to_all(spectra.reshape(nfreq, 1, rows, 1, npts), 'blk', split_axi...  25.2 us
    all_to_all x1, blocking collectives, body(): parts = lax.all_to_all(gram, 'pts', split_axis=0, concat_axis=0, tiled=True)  18.5 us
    pallas_call x1, Pallas kernels, body(): pl.pallas_call(modes_kernel, out_shape=[jax.ShapeDtypeStruct((nblocks * 2...  11.5 us
    ppermute x1, starting transfers between devices, body(): tail = lax.ppermute(tail, 'blk', [(i + 1, i) for i in range(nblocks - 1)])  8.79 us
    pallas_call x2, Pallas kernels, half_spectra(): pl.pallas_call(functools.partial(half_spectra_kernel, tail, nvars), out_s...  4.35 us
  transfers between devices with their start and end apart: 1, of which 0 were waited for; matrix products, arithmetic and copies ran while one was open for 0% of the time, Pallas kernels for 3%

profile of v4, /device:TPU:1, one launch (start us, length us, event | category | flops | bytes accessed | tf_op | source)
XLA Modules:
  0.0 69.8 jit_solution(12363981370298988049)
XLA Ops:
  0.6 0.0 copy-start
  0.6 0.0 copy-start.2
  0.6 0.0 copy-start.3
  0.7 2.5 %tail.1 = f32[640,128]{1,0:T(8,128)} custom-call(s32[1,64]{1,0:T(1,128)} %bitcast.13, s32[1,64]{1,0:T(1,128)} %bitcast.15, f32[5,256,128]{2,1,0:T(8,128)} %bitcast.10), custom_call_target="tpu_custom_call" | custom-call | flops 251658240 | bytes 655360 | tf_op jit(solution)/shard_map/tail/pallas_call | solution.py:269
  3.2 0.0 copy-start.1
  3.2 8.8 %collective-permute-start = (f32[640,128]{1,0:T(8,128)}, f32[640,128]{1,0:T(8,128)S(1)}, u32[]{:S(2)}, u32[]{:S(2)}) collective-permute-start(f32[640,128]{1,0:T(8,128)} %tail.1), channel_id=1, source_target_pairs={{8,0},{16,8},{24,16},{32,24},{40,32},{48,40},{56,48},{64,56},{72,6... | collective-permute-start | bytes 983048 | tf_op jit(solution)/shard_map/ppermute | solution.py:295
  12.0 0.0 copy-done
  12.0 0.0 copy-done.2
  12.0 0.0 copy-done.3
  12.1 1.8 %head.1.head_ref = f32[640,128]{1,0:T(8,128)S(1)} custom-call(s32[1,64]{1,0:T(1,128)S(1)} %bitcast.14, s32[1,64]{1,0:T(1,128)S(1)} %bitcast.16, f32[5,256,128]{2,1,0:T(8,128)S(1)} %bitcast.11), custom_call_target="tpu_custom_call" | custom-call | flops 251658240 | bytes 655360 | tf_op jit(solution)/shard_map/head/pallas_call | solution.py:269
  13.9 0.0 collective-permute-done.tail_ref
  13.9 0.0 copy-done.1
  13.9 0.1 join.1
  14.0 25.2 %all_to_all.14 = f32[64,1,11,1,128]{4,3,2,1,0:T(1,128)S(1)} all-to-all(f32[64,1,11,1,128]{4,3,2,1,0:T(1,128)S(1)} %bitcast.12), channel_id=1, replica_groups=mesh['blk'=64,'pts'=8] {'blk'}, dimensions={0} | all-to-all | bytes 720896 | tf_op jit(solution)/shard_map/all_to_all | solution.py:304
  39.1 0.6 gram.1
  39.8 18.5 %all_to_all.15.parts_ref = f32[8,40,128]{2,1,0:T(8,128)S(1)} all-to-all(f32[8,40,128]{2,1,0:T(8,128)S(1)} %gram.1), channel_id=1, replica_groups=mesh['blk'=64,'pts'=8] {'pts'}, dimensions={0} | all-to-all | bytes 327680 | tf_op jit(solution)/shard_map/all_to_all | solution.py:313
  58.3 11.5 %modes.1 = (f32[640,128]{1,0:T(8,128)}, f32[1,64]{1,0:T(1,128)}) custom-call(f32[8,40,128]{2,1,0:T(8,128)S(1)} %all_to_all.15.parts_ref, f32[704,128]{1,0:T(8,128)S(1)} %bitcast.9), custom_call_target="tpu_custom_call" | custom-call | tf_op jit(solution)/shard_map/modes/pallas_call | solution.py:314
Async XLA Ops:
  0.6 11.4 %copy-start = (f32[256,5,128]{2,0,1:T(8,128)S(1)}, f32[256,5,128]{2,0,1:T(8,128)}, u32[]{:S(2)}) copy-start(f32[256,5,128]{2,0,1:T(8,128)} %param.4) | copy-start | bytes 1966084
  0.6 11.4 %copy-start.2 = (s32[64]{0:T(128)S(1)}, s32[64]{0:T(128)}, u32[]{:S(2)}) copy-start(s32[64]{0:T(128)} %param.6) | copy-start | bytes 772
  0.6 11.4 %copy-start.3 = (s32[64]{0:T(128)S(1)}, s32[64]{0:T(128)}, u32[]{:S(2)}) copy-start(s32[64]{0:T(128)} %param.7) | copy-start | bytes 772
  3.2 10.7 %copy-start.1 = (f32[5,128]{1,0:T(8,128)S(1)}, f32[5,128]{1,0:T(8,128)}, u32[]{:S(2)}) copy-start(f32[5,128]{1,0:T(8,128)} %weights_ref.3) | copy-start | bytes 7684
  3.2 10.6 %collective-permute-start = (f32[640,128]{1,0:T(8,128)}, f32[640,128]{1,0:T(8,128)S(1)}, u32[]{:S(2)}, u32[]{:S(2)}) collective-permute-start(f32[640,128]{1,0:T(8,128)} %tail.1), channel_id=1, source_target_pairs={{8,0},{16,8},{24,16},{32,24},{40,32},{48,40},{56,48},{64,56},{72,6... | collective-permute-start | bytes 983048 | tf_op jit(solution)/shard_map/ppermute | solution.py:295

commit v5 on v4

--- a/solution.py
+++ b/solution.py
@@ -276,7 +276,7 @@
             pltpu.VMEM((nvars, nfft, npts), F32),
             pltpu.SemaphoreType.DMA((nvars + 2,)),
         ],
-        compiler_params=pltpu.CompilerParams(vmem_limit_bytes=(60 if tail else 16) << 20),
+        compiler_params=pltpu.CompilerParams(vmem_limit_bytes=16 << 20),
         cost_estimate=pl.CostEstimate(flops=12 * NB * 2 * nfft * nvars * npts, bytes_accessed=4 * own.size, transcendentals=0),
         name="tail" if tail else "head",
     )(offsets, freqs, own)
@@ -291,7 +291,7 @@
     own = jnp.transpose(snapshots, (1, 0, 2))
     freqs = freqs.reshape(1, nfreq)
     offsets = offsets.reshape(1, nblocks)
-    tail = half_spectra(True, offsets, freqs, own)
+    tail = half_spectra(True, *(pltpu.with_memory_space_constraint(x, pltpu.HBM) for x in (offsets, freqs, own)))
     tail = lax.ppermute(tail, "blk", [(i + 1, i) for i in range(nblocks - 1)])
     head = half_spectra(False, offsets, freqs, own)
     scale = 1.0 / (nblocks * nvars * npts * nparts)

time: 70.4 us -> 69.4 us (0.986)
    pallas_call x2, Pallas kernels: 4.35 us -> 3.63 us  [half_spectra(): pl.pallas_call(functools.partial(half_spectra_kernel, tail, nvars), out_s...]
where the time goes in v5:
time: 69.4 us; the launch traced here: 68.9 us
  blocking collectives  43.5 us (63%)
  Pallas kernels  15.9 us (23%)
  starting transfers between devices  8.79 us (13%)
  between operations  0.73 us (1%)
    all_to_all x1, blocking collectives, body(): lax.all_to_all(spectra.reshape(nfreq, 1, rows, 1, npts), 'blk', split_axi...  25 us
    all_to_all x1, blocking collectives, body(): parts = lax.all_to_all(gram, 'pts', split_axis=0, concat_axis=0, tiled=True)  18.5 us
    pallas_call x1, Pallas kernels, body(): pl.pallas_call(modes_kernel, out_shape=[jax.ShapeDtypeStruct((nblocks * 2...  11.5 us
    ppermute x1, starting transfers between devices, body(): tail = lax.ppermute(tail, 'blk', [(i + 1, i) for i in range(nblocks - 1)])  8.79 us
    pallas_call x2, Pallas kernels, half_spectra(): pl.pallas_call(functools.partial(half_spectra_kernel, tail, nvars), out_s...  3.63 us
  transfers between devices with their start and end apart: 1, of which 0 were waited for; matrix products, arithmetic and copies ran while one was open for 0% of the time, Pallas kernels for 3%

profile of v5, /device:TPU:1, one launch (start us, length us, event | category | flops | bytes accessed | tf_op | source)
XLA Modules:
  0.0 68.9 jit_solution(8182622850565497365)
XLA Ops:
  0.6 0.0 copy-start
  0.6 0.0 copy-start.2
  0.7 0.0 copy-start.3
  0.7 1.8 %tail.1 = f32[640,128]{1,0:T(8,128)S(1)} custom-call(s32[1,64]{1,0:T(1,128)} %bitcast.13, s32[1,64]{1,0:T(1,128)} %bitcast.15, f32[5,256,128]{2,1,0:T(8,128)} %bitcast.10), custom_call_target="tpu_custom_call" | custom-call | flops 251658240 | bytes 655360 | tf_op jit(solution)/shard_map/tail/pallas_call | solution.py:269
  2.5 0.0 copy-start.1
  2.5 8.8 %collective-permute-start = (f32[640,128]{1,0:T(8,128)S(1)}, f32[640,128]{1,0:T(8,128)S(1)}, u32[]{:S(2)}, u32[]{:S(2)}) collective-permute-start(f32[640,128]{1,0:T(8,128)S(1)} %tail.1), channel_id=1, source_target_pairs={{8,0},{16,8},{24,16},{32,24},{40,32},{48,40},{56,48},{64,56},{72,6... | collective-permute-start | bytes 983048 | tf_op jit(solution)/shard_map/ppermute | solution.py:295
  11.3 0.0 copy-done
  11.3 0.0 copy-done.2
  11.3 0.0 copy-done.3
  11.3 1.8 %head.1.head_ref = f32[640,128]{1,0:T(8,128)S(1)} custom-call(s32[1,64]{1,0:T(1,128)S(1)} %bitcast.14, s32[1,64]{1,0:T(1,128)S(1)} %bitcast.16, f32[5,256,128]{2,1,0:T(8,128)S(1)} %bitcast.11), custom_call_target="tpu_custom_call" | custom-call | flops 251658240 | bytes 655360 | tf_op jit(solution)/shard_map/head/pallas_call | solution.py:269
  13.1 0.0 collective-permute-done.tail_ref
  13.2 0.0 copy-done.1
  13.2 0.1 join.1
  13.2 25.0 %all_to_all.14 = f32[64,1,11,1,128]{4,3,2,1,0:T(1,128)S(1)} all-to-all(f32[64,1,11,1,128]{4,3,2,1,0:T(1,128)S(1)} %bitcast.12), channel_id=1, replica_groups=mesh['blk'=64,'pts'=8] {'blk'}, dimensions={0} | all-to-all | bytes 720896 | tf_op jit(solution)/shard_map/all_to_all | solution.py:304
  38.2 0.6 gram.1
  38.8 18.5 %all_to_all.15.parts_ref = f32[8,40,128]{2,1,0:T(8,128)S(1)} all-to-all(f32[8,40,128]{2,1,0:T(8,128)S(1)} %gram.1), channel_id=1, replica_groups=mesh['blk'=64,'pts'=8] {'pts'}, dimensions={0} | all-to-all | bytes 327680 | tf_op jit(solution)/shard_map/all_to_all | solution.py:313
  57.4 11.5 %modes.1 = (f32[640,128]{1,0:T(8,128)}, f32[1,64]{1,0:T(1,128)}) custom-call(f32[8,40,128]{2,1,0:T(8,128)S(1)} %all_to_all.15.parts_ref, f32[704,128]{1,0:T(8,128)S(1)} %bitcast.9), custom_call_target="tpu_custom_call" | custom-call | tf_op jit(solution)/shard_map/modes/pallas_call | solution.py:314
Async XLA Ops:
  0.6 10.7 %copy-start = (f32[256,5,128]{2,0,1:T(8,128)S(1)}, f32[256,5,128]{2,0,1:T(8,128)}, u32[]{:S(2)}) copy-start(f32[256,5,128]{2,0,1:T(8,128)} %param.4) | copy-start | bytes 1966084
  0.6 10.7 %copy-start.2 = (s32[64]{0:T(128)S(1)}, s32[64]{0:T(128)}, u32[]{:S(2)}) copy-start(s32[64]{0:T(128)} %param.6) | copy-start | bytes 772
  0.7 10.7 %copy-start.3 = (s32[64]{0:T(128)S(1)}, s32[64]{0:T(128)}, u32[]{:S(2)}) copy-start(s32[64]{0:T(128)} %param.7) | copy-start | bytes 772
  2.5 10.7 %copy-start.1 = (f32[5,128]{1,0:T(8,128)S(1)}, f32[5,128]{1,0:T(8,128)}, u32[]{:S(2)}) copy-start(f32[5,128]{1,0:T(8,128)} %weights_ref.3) | copy-start | bytes 7684
  2.5 10.6 %collective-permute-start = (f32[640,128]{1,0:T(8,128)S(1)}, f32[640,128]{1,0:T(8,128)S(1)}, u32[]{:S(2)}, u32[]{:S(2)}) collective-permute-start(f32[640,128]{1,0:T(8,128)S(1)} %tail.1), channel_id=1, source_target_pairs={{8,0},{16,8},{24,16},{32,24},{40,32},{48,40},{56,48},{64,56},{72,6... | collective-permute-start | bytes 983048 | tf_op jit(solution)/shard_map/ppermute | solution.py:295
